TPU v7x, 32 devices: a whole 2x2x4 slice. The times are simulated.
32 devices in a mesh: tm: 16 (over z, x, core), space: 2 (over y).
Axes of the slice: x: 2, y: 2, z: 4, core: 2. Of those that a mesh axis runs over, the one named last changes fastest.
Arguments:
- conv_input: bfloat16 [16, 12, 40, 256], P('tm', None, 'space'), may hold values from -6 to 6
- conv_out: bfloat16 [16, 12, 40, 256], P('tm', None, 'space'), may hold values from -20 to 20
- kernel: bfloat16 [3, 3, 3, 256, 256], replicated, may hold values from -0.078125 to 0.078125
- gain: float32 [256], replicated, may hold values from 0.25 to 1.75
- bias: float32 [256], replicated, may hold values from -4 to 4
- cotangent: bfloat16 [16, 12, 40, 256], P('tm', None, 'space'), may hold values from -7 to 7
Outputs:
- grad_input: bfloat16 [16, 12, 40, 256], P('tm', None, 'space')
- grad_kernel: float32 [3, 3, 3, 256, 256], P(None, None, None, None, 'space')
- grad_gain: float32 [256], replicated
- grad_bias: float32 [256], replicated
All inputs are finite; a program needn't handle non-finite values.
Results may differ from a plain program's by a relative error of at most 0.0075.
Values may be sent and summed in bfloat16 or wider, within the bound.
A program may use at most 64 MiB of HBM per device.

v0:
```python
import functools

import jax
import jax.numpy as jnp
from jax import lax
from jax.experimental import pallas as pl
from jax.experimental.pallas import tpu as pltpu
from jax.sharding import PartitionSpec as P

GROUPS = 32
STREAMS = 6
PARTS = 2
EPSILON = 1e-06
MESH = pl.DeviceIdType.MESH
F32 = jnp.float32
BF16 = jnp.bfloat16


def round_up(value, unit):
    return (value + unit - 1) // unit * unit


def group_sum(x, width):
    lanes = x.shape[1]
    lane = lax.broadcasted_iota(jnp.int32, x.shape, 1)
    step = 1
    while step < width:
        up = pltpu.roll(x, lanes - step, 1)
        down = pltpu.roll(x, step, 1)
        x = x + jnp.where((lane // step) % 2 == 0, up, down)
        step *= 2
    return x


def hand_out(gi_in, gk_in, gg_in, gb_in, gi_out, gk_out, gg_out, gb_out):
    gk_out[...] = gk_in[...].astype(F32)

    @pl.when(pl.program_id(0) == 0)
    def _():
        gi_out[...] = gi_in[...]
        gg_out[...] = gg_in[...]
        gb_out[...] = gb_in[...]


def body(
    T, S, sizes,
    x_hbm, co_hbm, k_ref, gain_ref, bias_ref, ct_hbm,
    gi_ref, gk_ref, gg_ref, gb_ref,
    x_ref, co_ref, ct_ref, strip, edge_out, edge_in, slice_out, slice_in, x_in,
    st_out, st_in, fbuf, gown, gwide, xt, wbuf, acc, sbuf, rbuf,
    in_sem, w_sem, st_send, st_recv, bulk_send, bulk_recv, rs_send, rs_recv,
):
    N = T * S
    total_rows = sum(sizes)
    _, rows, cols, chans = co_ref.shape
    ce = chans // S
    pitch = fbuf.shape[1]
    flat = rows * pitch
    flat_all = (rows + 2) * pitch
    halves = chans // 128
    t = lax.axis_index("tm")
    s = lax.axis_index("space")
    me = t * S + s

    loads = [
        pltpu.make_async_copy(src, dst, in_sem.at[i])
        for i, (src, dst) in enumerate(((co_hbm, co_ref), (ct_hbm, ct_ref), (x_hbm, x_ref)))
    ]
    for copy in loads:
        copy.start()
    load = pltpu.make_async_copy(k_ref, wbuf, w_sem)
    load.start()

    barrier = pltpu.get_barrier_semaphore()

    def greet(r, carry):
        d = lax.rem(me + r, N)
        pl.semaphore_signal(barrier, inc=1, device_id=(d // S, lax.rem(d, S)), device_id_type=MESH)
        return carry

    lax.fori_loop(1, N, greet, 0)

    for copy in loads:
        copy.wait()
    for arr, ref in ((0, co_ref), (1, ct_ref)):
        whole = ref[0]
        for h in range(rows):
            edge_out[0, arr, h : h + 1, :] = whole[h, 0:1, :]
            edge_out[1, arr, h : h + 1, :] = whole[h, cols - 1 : cols, :]
        for j in range(S):
            slice_out[j, arr] = whole[:, :, j * ce : (j + 1) * ce]
    conv = co_ref[0].astype(F32)
    first = jnp.sum(jnp.sum(conv, axis=0), axis=0, keepdims=True)
    second = jnp.sum(jnp.sum(conv * conv, axis=0), axis=0, keepdims=True)

    def put_stats(which, one, two):
        for i in range(halves):
            st_out[which, i : i + 1, :] = one[:, i * 128 : (i + 1) * 128]
            st_out[which, halves + i : halves + i + 1, :] = two[:, i * 128 : (i + 1) * 128]

    def send_stats(which):
        def send(r, carry):
            r = 1 + lax.rem(r + N // 2 - 1, N - 1)
            d = lax.rem(me + r, N)
            pltpu.make_async_remote_copy(
                src_ref=st_out.at[which], dst_ref=st_in.at[which, r - 1],
                send_sem=st_send.at[which], recv_sem=st_recv.at[which],
                device_id=(d // S, lax.rem(d, S)), device_id_type=MESH,
            ).start()
            return carry

        lax.fori_loop(1, N, send, 0)

    def take_stats(which):
        pltpu.make_async_copy(st_in.at[which], st_in.at[which], st_recv.at[which]).wait()
        return jnp.sum(st_in[which], axis=0) + st_out[which]

    put_stats(0, first, second)
    pl.semaphore_wait(barrier, N - 1)
    send_stats(0)

    bulk = []

    def push(src, dst, device):
        i = len(bulk)
        copy = pltpu.make_async_remote_copy(
            src_ref=src, dst_ref=dst, send_sem=bulk_send.at[i], recv_sem=bulk_recv.at[i],
            device_id=device, device_id_type=MESH,
        )
        copy.start()
        bulk.append(copy)

    back = lax.rem(t + T - 1, T)
    for arr, ref in ((0, co_ref), (1, ct_ref)):
        push(ref.at[0], strip.at[0, arr], (back, s))
    for r in range(1, S):
        other = lax.rem(s + S - r, S)
        push(slice_out.at[other], slice_in.at[0, r - 1], (t, other))
    relayed = len(bulk)
    for k in range(3):
        tk = lax.rem(t + T - k, T)
        push(edge_out.at[1], edge_in.at[k, 0], (tk, lax.rem(s + 1, S)))
        push(edge_out.at[0], edge_in.at[k, 1], (tk, lax.rem(s + S - 1, S)))
    for r in range(1, S):
        push(x_ref.at[0], x_in.at[r - 1], (t, lax.rem(s + S - r, S)))
    direct = len(bulk)

    def relay_first():
        for arr in range(2):
            bulk[arr].wait_recv()
            push(strip.at[0, arr], strip.at[1, arr], (back, s))
        for r in range(1, S):
            bulk[1 + r].wait_recv()
            push(slice_in.at[0, r - 1], slice_in.at[1, r - 1], (back, s))

    def relay_second():
        for r in range(1, S):
            bulk[direct + 1 + r].wait_recv()
            push(slice_in.at[1, r - 1], slice_in.at[2, r - 1], (back, s))

    fbuf[...] = jnp.zeros_like(fbuf)

    def put_input(index, value):
        fbuf[1 : rows + 1, 0:cols, :] = value.astype(F32)
        placed = fbuf[1 : rows + 1].reshape(flat, chans)
        xt[index] = jnp.transpose(placed).astype(BF16)

    put_input(0, x_ref[0])
    if total_rows > 27 * chans:
        acc[27 * chans :, :] = jnp.zeros((total_rows - 27 * chans, ce), F32)

    gain = gain_ref[...]
    bias = bias_ref[...]
    width = chans // GROUPS
    count = rows * cols * width * N
    relay_first()
    sums = take_stats(0)
    grouped = group_sum(sums, width)
    mean2 = grouped[:halves] / count
    inv2 = lax.rsqrt(grouped[halves:] / count - mean2 * mean2 + EPSILON)

    def wide(two):
        return jnp.concatenate([two[i : i + 1] for i in range(halves)], axis=1)

    mean, inv = wide(mean2), wide(inv2)

    def shift_grad(conv, cot, mean, inv, gain, bias):
        normed = (conv.astype(F32) - mean) * inv
        shifted = normed * gain + bias
        sigma = jax.nn.sigmoid(shifted)
        return normed, cot.astype(F32) * sigma * (1.0 + shifted * (1.0 - sigma))

    normed, grad = shift_grad(co_ref[0], ct_ref[0], mean, inv, gain, bias)
    put_stats(
        1,
        jnp.sum(jnp.sum(grad, axis=0), axis=0, keepdims=True),
        jnp.sum(jnp.sum(grad * normed, axis=0), axis=0, keepdims=True),
    )
    send_stats(1)
    relay_second()
    for copy in bulk[relayed:direct]:
        copy.wait_recv()
    for r in range(1, S):
        put_input(r, x_in[r - 1])
    for copy in bulk[direct : direct + 2] + bulk[direct + 1 + S :]:
        copy.wait_recv()
    sums = take_stats(1)
    chan_bias, chan_gain = wide(sums[:halves]), wide(sums[halves:])
    gb_ref[...] = chan_bias
    gg_ref[...] = chan_gain
    gain2 = jnp.concatenate([gain[:, i * 128 : (i + 1) * 128] for i in range(halves)], axis=0)
    plain = wide(group_sum(sums[:halves] * gain2, width)) / count
    product = wide(group_sum(sums[halves:] * gain2, width)) / count

    def conv_grad(conv, cot, params):
        mean, inv, gain, bias, plain, product = params
        normed, grad = shift_grad(conv, cot, mean, inv, gain, bias)
        return inv * (grad * gain - plain - normed * product)

    def part(v):
        out = v[..., 0:ce]
        for j in range(1, S):
            out = jnp.where(s == j, v[..., j * ce : (j + 1) * ce], out)
        return out

    params = (mean, inv, gain, bias, plain, product)
    own_params = tuple(part(p) for p in params)

    def shifts(f):
        n = f.shape[0]
        return (pltpu.roll(f, n - 1, 0), f, pltpu.roll(f, 1, 0))

    for k in range(3):
        live = t + k < T
        conv, cot = (co_ref[0], ct_ref[0]) if k == 0 else (strip[k - 1, 0], strip[k - 1, 1])
        g = jnp.where(live, conv_grad(conv, cot, params), 0.0)
        fbuf[1 : rows + 1, 0:cols, :] = g
        left = jnp.where(live & (s > 0), conv_grad(edge_in[k, 0, 0], edge_in[k, 0, 1], params), 0.0)
        right = jnp.where(live & (s < S - 1), conv_grad(edge_in[k, 1, 0], edge_in[k, 1, 1], params), 0.0)
        for h in range(rows):
            fbuf[h, pitch - 1 : pitch, :] = left[h : h + 1]
            fbuf[h + 1, cols : cols + 1, :] = right[h : h + 1]
        f = fbuf[...].reshape(flat_all, chans)
        for c, w in enumerate(shifts(f)):
            gown[k, :, c * chans : (c + 1) * chans] = w.astype(BF16)
            gwide[0, k, :, c * ce : (c + 1) * ce] = part(w).astype(BF16)
        near = [part(g)] + [
            jnp.where(live, conv_grad(slice_in[k, r - 1, 0], slice_in[k, r - 1, 1], own_params), 0.0)
            for r in range(1, S)
        ]
        for r in range(1, S):
            j = lax.rem(s + r, S)
            before, after = near[r - 1], near[(r + 1) % S]
            fbuf[1 : rows + 1, 0:cols, 0:ce] = near[r]
            fbuf[0:rows, pitch - 1 : pitch, 0:ce] = jnp.where(j > 0, before[:, cols - 1 : cols, :], 0.0)
            fbuf[1 : rows + 1, cols : cols + 1, 0:ce] = jnp.where(j < S - 1, after[:, 0:1, :], 0.0)
            f = fbuf[:, :, 0:ce].reshape(flat_all, ce)
            for c, w in enumerate(shifts(f)):
                gwide[r, k, :, c * ce : (c + 1) * ce] = w.astype(BF16)

    bits = T.bit_length() - 1
    straight = list(range(bits))
    swapped = list(range(bits))
    if bits > 2:
        swapped[1], swapped[2] = swapped[2], swapped[1]
    streams = len(sizes)
    orders = [(straight, swapped)[p % 2] for p in range(streams)]
    bases = [sum(sizes[:p]) for p in range(streams)]
    offs = [0] * streams
    flying = [None] * streams
    copies = []

    def side(bit):
        return lax.rem(t // (2**bit), 2)

    def partner(bit):
        return (t + (1 - 2 * side(bit)) * 2**bit, s)

    def span(p, off, n):
        return pl.ds(pl.multiple_of(bases[p] + off, 16), n)

    def begin(i, p):
        half = sizes[p] >> (i + 1)
        start = bases[p] + sizes[p] - (sizes[p] >> i)
        bit = orders[p][i]
        mine = side(bit)
        sbuf[start : start + half, :] = acc[span(p, offs[p] + (1 - mine) * half, half), :].astype(BF16)
        copy = pltpu.make_async_remote_copy(
            src_ref=sbuf.at[start : start + half], dst_ref=rbuf.at[start : start + half],
            send_sem=rs_send.at[0, p, i], recv_sem=rs_recv.at[0, p, i],
            device_id=partner(bit), device_id_type=MESH,
        )
        copy.start()
        copies.append(copy)
        offs[p] = offs[p] + mine * half
        flying[p] = copy

    def finish(i, p):
        half = sizes[p] >> (i + 1)
        start = bases[p] + sizes[p] - (sizes[p] >> i)
        flying[p].wait_recv()
        at = span(p, offs[p], half)
        acc[at, :] = acc[at, :] + rbuf[start : start + half, :].astype(F32)

    def input_grad(a, total):
        for b in range(3):
            for c in range(3):
                term = lax.dot_general(
                    gown[2 - a, (2 - b) * pitch : (2 - b) * pitch + flat, c * chans : (c + 1) * chans],
                    wbuf[a, b, c], (((1,), (1,)), ((), ())), preferred_element_type=F32,
                )
                total = term if total is None else total + term
        return total

    started = 0
    for a in range(3):
        for b in range(3):
            res = None
            for j in range(S):
                term = jnp.dot(
                    xt[j], gwide[j, 2 - a, (2 - b) * pitch : (2 - b) * pitch + flat, :],
                    preferred_element_type=F32,
                )
                res = term if res is None else res + term
            for c in range(3):
                at = ((a * 3 + b) * 3 + c) * chans
                acc[at : at + chans, :] = res[:, c * ce : (c + 1) * ce]
            done = total_rows if a * 3 + b == 8 else ((a * 3 + b) * 3 + 3) * chans
            while started < streams and bases[started] + sizes[started] <= done:
                begin(0, started)
                started += 1

    load.wait()
    total = None
    for i in range(bits):
        for p in range(streams):
            finish(i, p)
            if i + 1 < bits:
                begin(i + 1, p)
        if i == 0:
            for a in range(3):
                total = input_grad(a, total)
            gi_ref[0] = total.reshape(rows, pitch, chans)[:, 0:cols, :].astype(BF16)

    def spread(i, p):
        n = sizes[p] >> (i + 1)
        bit = orders[p][i]
        at = span(p, offs[p], n)
        copy = pltpu.make_async_remote_copy(
            src_ref=gk_ref.at[at], dst_ref=gk_ref.at[at],
            send_sem=rs_send.at[1, p, i], recv_sem=rs_recv.at[1, p, i],
            device_id=partner(bit), device_id_type=MESH,
        )
        copy.start()
        copies.append(copy)
        offs[p] = offs[p] - side(bit) * n
        flying[p] = copy

    for p in range(streams):
        at = span(p, offs[p], sizes[p] >> bits)
        gk_ref[at, :] = acc[at, :].astype(BF16)
        spread(bits - 1, p)
    for i in reversed(range(bits)):
        for p in range(streams):
            flying[p].wait_recv()
            if i > 0:
                spread(i - 1, p)

    for copy in copies:
        copy.wait_send()
    for copy in bulk:
        copy.wait_send()
    for which in range(2):
        pltpu.make_async_copy(st_in.at[which], st_in.at[which], st_send.at[which]).wait()


def solution(mesh):
    T, S = mesh.shape["tm"], mesh.shape["space"]

    def shards(conv_input, conv_out, kernel, gain, bias, cotangent):
        _, rows, cols, chans = conv_out.shape
        ce = chans // S
        bits = T.bit_length() - 1
        groups = round_up(27 * chans, T * 16) // (T * 16)
        streams = min(STREAMS, groups)
        sizes = [(groups // streams + (p < groups % streams)) * T * 16 for p in range(streams)]
        total_rows = sum(sizes)
        pitch = round_up(cols + 2, 16)
        n_bulk = 3 * (2 + S - 1) + (S - 1) + 4
        vmem = pl.BlockSpec(memory_space=pltpu.VMEM)
        whole = pl.BlockSpec(memory_space=pl.ANY)
        gi, gk, gg, gb = pl.pallas_call(
            functools.partial(body, T, S, sizes),
            out_shape=(
                jax.ShapeDtypeStruct(conv_input.shape, BF16),
                jax.ShapeDtypeStruct((total_rows, ce), BF16),
                jax.ShapeDtypeStruct((1, chans), F32),
                jax.ShapeDtypeStruct((1, chans), F32),
            ),
            in_specs=[whole, whole, whole, vmem, vmem, whole],
            out_specs=(vmem, vmem, vmem, vmem),
            scratch_shapes=[
                pltpu.VMEM(conv_input.shape, BF16),
                pltpu.VMEM(conv_out.shape, BF16),
                pltpu.VMEM(cotangent.shape, BF16),
                pltpu.VMEM((2, 2, rows, cols, chans), BF16),
                pltpu.VMEM((2, 2, rows, chans), BF16),
                pltpu.VMEM((3, 2, 2, rows, chans), BF16),
                pltpu.VMEM((S, 2, rows, cols, ce), BF16),
                pltpu.VMEM((3, S - 1, 2, rows, cols, ce), BF16),
                pltpu.VMEM((S - 1, rows, cols, chans), BF16),
                pltpu.VMEM((2, 2 * chans // 128, 128), F32),
                pltpu.VMEM((2, T * S - 1, 2 * chans // 128, 128), F32),
                pltpu.VMEM((rows + 2, pitch, chans), F32),
                pltpu.VMEM((3, (rows + 2) * pitch, 3 * chans), BF16),
                pltpu.VMEM((S, 3, (rows + 2) * pitch, 3 * ce), BF16),
                pltpu.VMEM((S, chans, rows * pitch), BF16),
                pltpu.VMEM((3, 3, 3, chans, chans), BF16),
                pltpu.VMEM((total_rows, ce), F32),
                pltpu.VMEM((total_rows, ce), BF16),
                pltpu.VMEM((total_rows, ce), BF16),
                pltpu.SemaphoreType.DMA((3,)),
                pltpu.SemaphoreType.DMA,
                pltpu.SemaphoreType.DMA((2,)),
                pltpu.SemaphoreType.DMA((2,)),
                pltpu.SemaphoreType.DMA((n_bulk,)),
                pltpu.SemaphoreType.DMA((n_bulk,)),
                pltpu.SemaphoreType.DMA((2, streams, bits)),
                pltpu.SemaphoreType.DMA((2, streams, bits)),
            ],
            compiler_params=pltpu.CompilerParams(
                collective_id=0, has_side_effects=True, vmem_limit_bytes=60 * 1024 * 1024
            ),
        )(conv_input, conv_out, kernel, gain.reshape(1, chans), bias.reshape(1, chans), cotangent)
        part_rows = 27 * chans // PARTS
        gi, gk, gg, gb = pl.pallas_call(
            hand_out,
            grid=(PARTS,),
            out_shape=(
                jax.ShapeDtypeStruct(gi.shape, BF16),
                jax.ShapeDtypeStruct((27 * chans, ce), F32),
                jax.ShapeDtypeStruct((1, chans), F32),
                jax.ShapeDtypeStruct((1, chans), F32),
            ),
            in_specs=[
                pl.BlockSpec(gi.shape, lambda i: (0, 0, 0, 0)),
                pl.BlockSpec((part_rows, ce), lambda i: (i, 0)),
                pl.BlockSpec((1, chans), lambda i: (0, 0)),
                pl.BlockSpec((1, chans), lambda i: (0, 0)),
            ],
            out_specs=(
                pl.BlockSpec(gi.shape, lambda i: (0, 0, 0, 0)),
                pl.BlockSpec((part_rows, ce), lambda i: (i, 0)),
                pl.BlockSpec((1, chans), lambda i: (0, 0)),
                pl.BlockSpec((1, chans), lambda i: (0, 0)),
            ),
        )(gi, gk, gg, gb)
        return gi, gk.reshape(3, 3, 3, chans, ce), gg.reshape(chans), gb.reshape(chans)

    strip = P("tm", None, "space", None)
    return jax.shard_map(
        shards,
        mesh=mesh,
        in_specs=(strip, strip, P(), P(), P(), strip),
        out_specs=(strip, P(None, None, None, None, "space"), P(), P()),
        check_vma=False,
    )
```

profile of v0, /device:TPU:0, one launch (start us, length us, event | category | flops | bytes accessed | tf_op | source)
XLA Modules:
  0.0 61.8 jit_solution(5925131388942344253)
XLA Ops:
  0.6 58.0 %shard_map.93 = (bf16[1,12,20,256]{3,2,1,0:T(8,128)(2,1)}, bf16[6912,128]{1,0:T(8,128)(2,1)}, f32[1,256]{1,0:T(1,128)}, f32[1,256]{1,0:T(1,128)}) custom-call(bf16[1,12,20,256]{3,2,1,0:T(8,128)(2,1)} %x_hbm.1, bf16[1,12,20,256]{3,2,1,0:T(8,128)(2,1)} %co_hbm.1, bf16[3,3,3,256,256]{4,3,2,1,0:T(8,128)(2,1)} %k_ref.1, f32[1,256]{1,0:T(1,128)} %bitcast.5, ...), custom_call_target="tpu_custom_call" | custom-call | tf_op jit(solution)/shard_map/pallas_call | solution.py:392
  58.6 3.2 %shard_map.94 = (bf16[1,12,20,256]{3,2,1,0:T(8,128)(2,1)}, f32[6912,128]{1,0:T(8,128)}, f32[1,256]{1,0:T(1,128)}, f32[1,256]{1,0:T(1,128)}) custom-call(bf16[1,12,20,256]{3,2,1,0:T(8,128)(2,1)} %get-tuple-element.12.gi_in, bf16[6912,128]{1,0:T(8,128)(2,1)} %get-tuple-element.13.gk_in, f32[1,256]{1,0:T(1,128)} %get-tuple-element.14.gg_in, ...), custom_call_target="tpu_custom_call" | custom-call | tf_op jit(solution)/shard_map/pallas_call | solution.py:436
where the time goes:
time: 63 us; the launch traced here: 61.8 us
  Pallas kernels  61.1 us (97%)
  between operations  0.64 us (1%)
    pallas_call x1, Pallas kernels, shards(): pl.pallas_call(functools.partial(body, T, S, sizes), out_shape=(jax.Shape...  58 us
    pallas_call x1, Pallas kernels, shards(): pl.pallas_call(hand_out, grid=(PARTS,), out_shape=(jax.ShapeDtypeStruct(g...  3.17 us

commit v1 on v0

v1 whole, which is shorter than its diff:
```python
import functools
import heapq

import jax
import jax.numpy as jnp
from jax import lax
from jax.experimental import pallas as pl
from jax.experimental.pallas import tpu as pltpu
from jax.sharding import PartitionSpec as P

GROUPS = 32
STREAMS = 9
PARTS = 4
EPSILON = 1e-06
MESH = pl.DeviceIdType.MESH
F32 = jnp.float32
BF16 = jnp.bfloat16


def round_up(value, unit):
    return (value + unit - 1) // unit * unit


def group_sum(x, width):
    lanes = x.shape[1]
    lane = lax.broadcasted_iota(jnp.int32, x.shape, 1)
    step = 1
    while step < width:
        up = pltpu.roll(x, lanes - step, 1)
        down = pltpu.roll(x, step, 1)
        x = x + jnp.where((lane // step) % 2 == 0, up, down)
        step *= 2
    return x


def hand_out(gi_in, gk_in, gg_in, gb_in, gi_out, gk_out, gg_out, gb_out):
    gk_out[...] = gk_in[...].astype(F32)

    @pl.when(pl.program_id(0) == 0)
    def _():
        gi_out[...] = gi_in[...]
        gg_out[...] = gg_in[...]
        gb_out[...] = gb_in[...]


TAPS_A = (2, 1, 0)
MATMUL = 0.36
FILLER = 0.36
ON_CHIP = (1.0, 250e3)
ON_LINK = (1.7, 42e3)
FAR = 0.75


def stage_orders(bits, streams):
    straight = list(range(bits))
    swapped = list(range(bits))
    if bits > 2:
        swapped[1], swapped[2] = swapped[2], swapped[1]
    return [swapped if p % 4 == 2 else straight for p in range(streams)]


def stream_starts(sizes, chans):
    done, begun, starts = set(), set(), []
    edges = [sum(sizes[:p]) for p in range(len(sizes) + 1)]
    for a in TAPS_A:
        for b in range(3):
            done.add(a * 3 + b)
            ready = []
            for p in range(len(sizes)):
                first, last = edges[p] // (3 * chans), (min(edges[p + 1], 27 * chans) - 1) // (3 * chans)
                if p not in begun and all(g in done for g in range(first, last + 1)):
                    begun.add(p)
                    ready.append(p)
            starts.append(((a, b), ready))
    return starts


def plan(bits, sizes, orders, starts, row_bytes):
    free = {}
    heap = []
    steps = 2 * bits

    def send(now, p, step):
        level = step if step < bits else steps - 1 - step
        rows = sizes[p] >> (level + 1)
        bit = orders[p][level]
        latency, rate = ON_CHIP if bit == 0 else ON_LINK
        time = rows * row_bytes / rate
        if bit > 2:
            latency, time = latency + FAR, 2 * time
        link = min(bit, 2)
        begin = max(now, free.get(link, 0.0))
        free[link] = begin + time
        heapq.heappush(heap, (begin + time + latency, step, p))

    matmuls = list(starts)
    fillers = [(0.0, ("gown", 0)), (4.5, ("gown", 1)), (7.5, ("gown", 2))]
    fillers += [(0.0, ("input", a, b)) for a in TAPS_A for b in range(3)]
    tasks, now = [], 0.0
    while heap or matmuls or fillers:
        if heap and heap[0][0] <= now:
            _, step, p = heapq.heappop(heap)
            tasks.append(("arrive", p, step))
            now += 0.03 + 1.5e-4 * (sizes[p] >> (step + 1) if step < bits else 0)
            if step + 1 < steps:
                send(now, p, step + 1)
        elif matmuls:
            (a, b), ready = matmuls.pop(0)
            tasks.append(("taps", a, b, ready))
            now += MATMUL
            for p in ready:
                send(now, p, 0)
        elif fillers and fillers[0][0] <= now:
            tasks.append(fillers.pop(0)[1])
            now += FILLER
        else:
            times = [heap[0][0]] if heap else []
            times += [fillers[0][0]] if fillers else []
            now = min(times)
    return tasks


def body(
    T, S, sizes,
    x_hbm, co_hbm, k_hbm, gain_ref, bias_ref, ct_hbm,
    gi_ref, gk_ref, gg_ref, gb_ref,
    xw, co_ref, ct_ref, slice_out, cw, st_out, st_in, own, pre, fx, fg, fbuf,
    gs, gh, ge_out, ge_in, gown, gw, xt, wbuf, tot, acc, sbuf, rbuf,
    in_sem, w_sem, st_send, st_recv, bulk_send, bulk_recv, rs_send, rs_recv,
):
    N = T * S
    total_rows = sum(sizes)
    _, rows, cols, chans = co_ref.shape
    width = cols * S
    ce = chans // S
    depth = xt.shape[2]
    pitch = fbuf.shape[1]
    flat = rows * pitch
    flat_all = (rows + 2) * pitch
    halves = chans // 128
    t = lax.axis_index("tm")
    s = lax.axis_index("space")
    me = t * S + s

    loads = [
        pltpu.make_async_copy(src, dst, in_sem.at[i])
        for i, (src, dst) in enumerate(((co_hbm, co_ref), (ct_hbm, ct_ref), (x_hbm.at[0], xw.at[0, s])))
    ]
    for copy in loads:
        copy.start()
    load = pltpu.make_async_copy(k_hbm, wbuf, w_sem)
    load.start()

    barrier = pltpu.get_barrier_semaphore()

    def greet(r, carry):
        d = lax.rem(me + r, N)
        pl.semaphore_signal(barrier, inc=1, device_id=(d // S, lax.rem(d, S)), device_id_type=MESH)
        return carry

    lax.fori_loop(1, N, greet, 0)

    loads[0].wait()
    conv = co_ref[0].astype(F32)
    first = jnp.sum(jnp.sum(conv, axis=0), axis=0, keepdims=True)
    second = jnp.sum(jnp.sum(conv * conv, axis=0), axis=0, keepdims=True)

    def put_stats(which, one, two):
        for i in range(halves):
            st_out[which, i : i + 1, :] = one[:, i * 128 : (i + 1) * 128]
            st_out[which, halves + i : halves + i + 1, :] = two[:, i * 128 : (i + 1) * 128]

    def send_stats(which):
        def send(r, carry):
            r = 1 + lax.rem(r + N // 2 - 1, N - 1)
            d = lax.rem(me + r, N)
            pltpu.make_async_remote_copy(
                src_ref=st_out.at[which], dst_ref=st_in.at[which, r - 1],
                send_sem=st_send.at[which], recv_sem=st_recv.at[which],
                device_id=(d // S, lax.rem(d, S)), device_id_type=MESH,
            ).start()
            return carry

        lax.fori_loop(1, N, send, 0)

    def take_stats(which):
        pltpu.make_async_copy(st_in.at[which], st_in.at[which], st_recv.at[which]).wait()
        return jnp.sum(st_in[which], axis=0) + st_out[which]

    put_stats(0, first, second)
    loads[1].wait()
    loads[2].wait()
    for arr, ref in ((0, co_ref), (1, ct_ref)):
        whole = ref[0]
        for j in range(S):
            slice_out[j, arr] = whole[:, :, j * ce : (j + 1) * ce]
    keep = pltpu.make_async_copy(slice_out.at[s], cw.at[s], in_sem.at[3])
    keep.start()
    pl.semaphore_wait(barrier, N - 1)
    send_stats(0)

    sent = []

    def push(src, dst, device, ok=None):
        i = len(sent)
        copy = pltpu.make_async_remote_copy(
            src_ref=src, dst_ref=dst, send_sem=bulk_send.at[i], recv_sem=bulk_recv.at[i],
            device_id=device, device_id_type=MESH,
        )
        if ok is None:
            copy.start()
        else:
            pl.when(ok)(copy.start)
        sent.append((copy, ok))
        return i

    def take(i, dst, ok=None):
        copy = pltpu.make_async_copy(dst, dst, bulk_recv.at[i])
        if ok is None:
            copy.wait()
        else:
            pl.when(ok)(copy.wait)

    def frame(n):
        return lax.rem(t + T + n, T)

    def strip(n):
        return lax.rem(s + S + n, S)

    ahead = (frame(1), s)
    behind = (frame(-1), s)
    has_next, has_before = t + 1 < T, t > 0
    cut, mate, past = [], [], [[], []]
    for r in range(1, S):
        cut.append(push(slice_out.at[strip(-r)], cw.at[s], (t, strip(-r))))
    past[0].append(push(xw.at[0, s], xw.at[1, s], ahead, has_next))
    for r in range(1, S):
        mate.append(push(xw.at[0, s], xw.at[0, s], (t, strip(-r))))

    def relay(k, r):
        j = strip(r)
        if k == 0:
            take(mate[r - 1], xw.at[0, j])
            ok = has_next
        else:
            take(past[k - 1][r], xw.at[k, j], has_before)
            ok = has_next & has_before
        if k < 2:
            past[k].append(push(xw.at[k, j], xw.at[k + 1, j], ahead, ok))

    fx[...] = jnp.zeros_like(fx)
    fg[...] = jnp.zeros_like(fg)
    fbuf[...] = jnp.zeros_like(fbuf)
    if total_rows > 27 * chans:
        acc[27 * chans :, :] = jnp.zeros((total_rows - 27 * chans, ce), F32)

    gain = gain_ref[...]
    bias = bias_ref[...]
    group = chans // GROUPS
    count = rows * width * T * group
    relay(1, 0)
    for r in range(1, S):
        relay(0, r)
    sums = take_stats(0)
    grouped = group_sum(sums, group)
    mean2 = grouped[:halves] / count
    inv2 = lax.rsqrt(grouped[halves:] / count - mean2 * mean2 + EPSILON)

    def wide(two):
        return jnp.concatenate([two[i : i + 1] for i in range(halves)], axis=1)

    mean, inv = wide(mean2), wide(inv2)

    def shift_grad(conv, cot, mean, inv, gain, bias):
        normed = (conv.astype(F32) - mean) * inv
        shifted = normed * gain + bias
        sigma = jax.nn.sigmoid(shifted)
        return normed, cot.astype(F32) * sigma * (1.0 + shifted * (1.0 - sigma))

    normed, grad = shift_grad(co_ref[0], ct_ref[0], mean, inv, gain, bias)
    own[0] = normed
    own[1] = grad
    put_stats(
        1,
        jnp.sum(jnp.sum(grad, axis=0), axis=0, keepdims=True),
        jnp.sum(jnp.sum(grad * normed, axis=0), axis=0, keepdims=True),
    )
    send_stats(1)

    def part(v):
        out = v[..., 0:ce]
        for j in range(1, S):
            out = jnp.where(s == j, v[..., j * ce : (j + 1) * ce], out)
        return out

    for r in range(1, S):
        relay(1, r)
        take(cut[r - 1], cw.at[strip(r)])
    keep.wait()
    firsts = tuple(part(p) for p in (mean, inv, gain, bias))
    for j in range(S):
        normed, grad = shift_grad(cw[j, 0], cw[j, 1], *firsts)
        pre[j, 0] = normed
        pre[j, 1] = grad

    def put_input(k):
        for j in range(S):
            value = xw[k, j].astype(F32)
            if k > 0:
                value = jnp.where(t >= k, value, 0.0)
            fx[0:rows, j * cols : (j + 1) * cols, :] = value
        placed = fx[...].reshape(fx.shape[0] * fx.shape[1], chans)[0:depth]
        xt[k] = jnp.transpose(placed).astype(BF16)

    put_input(0)
    put_input(1)
    relay_second = t > 1
    for r in range(S):
        take(past[1][r], xw.at[2, strip(r)], relay_second)
    put_input(2)
    sums = take_stats(1)
    chan_bias, chan_gain = wide(sums[:halves]), wide(sums[halves:])
    gb_ref[...] = chan_bias
    gg_ref[...] = chan_gain
    gain2 = jnp.concatenate([gain[:, i * 128 : (i + 1) * 128] for i in range(halves)], axis=0)
    plain = wide(group_sum(sums[:halves] * gain2, group)) / count
    product = wide(group_sum(sums[halves:] * gain2, group)) / count

    def conv_grad(normed, grad, inv, gain, plain, product):
        return inv * (grad * gain - plain - normed * product)

    g = conv_grad(own[0], own[1], inv, gain, plain, product)
    gs[...] = g.astype(BF16)
    for h in range(rows):
        ge_out[0, h : h + 1, :] = g[h, 0:1, :].astype(BF16)
        ge_out[1, h : h + 1, :] = g[h, cols - 1 : cols, :].astype(BF16)
    later = [push(gs, gh.at[0], behind, has_before)]
    rims = []
    for k in range(3):
        back = (frame(-k), strip(1)), (frame(-k), strip(-1))
        rims.append((
            push(ge_out.at[1], ge_in.at[k, 0], back[0], (t >= k) & (s + 1 < S)),
            push(ge_out.at[0], ge_in.at[k, 1], back[1], (t >= k) & (s > 0)),
        ))

    seconds = tuple(part(p) for p in (inv, gain, plain, product))
    for j in range(S):
        fg[1 : rows + 1, j * cols : (j + 1) * cols, :] = conv_grad(pre[j, 0], pre[j, 1], *seconds)
    tall = fg.shape[0] * width
    f = fg[...].reshape(tall, ce)
    column = lax.broadcasted_iota(jnp.int32, fg.shape, 1).reshape(tall, ce)
    moved = (
        jnp.where(column < width - 1, pltpu.roll(f, tall - 1, 0), 0.0),
        f,
        jnp.where(column > 0, pltpu.roll(f, 1, 0), 0.0),
    )
    for c, w in enumerate(moved):
        for b in range(3):
            gw[b, :, c * ce : (c + 1) * ce] = w[(2 - b) * width : (2 - b) * width + depth].astype(BF16)

    bits = T.bit_length() - 1
    streams = len(sizes)
    orders = stage_orders(bits, streams)
    starts = stream_starts(sizes, chans)
    bases = [sum(sizes[:p]) for p in range(streams)]
    offs = [0] * streams
    flying = [None] * streams
    copies = []

    def side(bit):
        return lax.rem(t // (2**bit), 2)

    def partner(bit):
        return (t + (1 - 2 * side(bit)) * 2**bit, s)

    def span(p, off, n):
        return pl.ds(pl.multiple_of(bases[p] + off, 16), n)

    def start_of(p, i):
        return bases[p] + sizes[p] - (sizes[p] >> i)

    def launch(i, p):
        half = sizes[p] >> (i + 1)
        start = start_of(p, i)
        copy = pltpu.make_async_remote_copy(
            src_ref=sbuf.at[start : start + half], dst_ref=rbuf.at[start : start + half],
            send_sem=rs_send.at[0, p, i], recv_sem=rs_recv.at[0, p, i],
            device_id=partner(orders[p][i]), device_id_type=MESH,
        )
        copy.start()
        copies.append(copy)
        flying[p] = copy

    def begin(p):
        half = sizes[p] >> 1
        mine = side(orders[p][0])
        start = start_of(p, 0)
        sbuf[start : start + half, :] = acc[span(p, (1 - mine) * half, half), :].astype(BF16)
        launch(0, p)
        offs[p] = mine * half

    def sum_at(p, i, off, n):
        at = span(p, offs[p] + off, n)
        seen = pl.ds(pl.multiple_of(start_of(p, i) + off, 16), n)
        return at, acc[at, :] + rbuf[seen, :].astype(F32)

    def spread(i, p):
        n = sizes[p] >> (i + 1)
        bit = orders[p][i]
        at = span(p, offs[p], n)
        copy = pltpu.make_async_remote_copy(
            src_ref=gk_ref.at[at], dst_ref=gk_ref.at[at],
            send_sem=rs_send.at[1, p, i], recv_sem=rs_recv.at[1, p, i],
            device_id=partner(bit), device_id_type=MESH,
        )
        copy.start()
        copies.append(copy)
        offs[p] = offs[p] - side(bit) * n
        flying[p] = copy

    def arrive(p, step):
        flying[p].wait_recv()
        if step < bits - 1:
            half = sizes[p] >> (step + 2)
            mine = side(orders[p][step + 1])
            start = start_of(p, step + 1)
            _, value = sum_at(p, step, (1 - mine) * half, half)
            sbuf[start : start + half, :] = value.astype(BF16)
            launch(step + 1, p)
            at, value = sum_at(p, step, mine * half, half)
            acc[at, :] = value
            offs[p] = offs[p] + mine * half
        elif step == bits - 1:
            at, value = sum_at(p, step, 0, sizes[p] >> bits)
            gk_ref[at, :] = value.astype(BF16)
            spread(bits - 1, p)
        elif step + 1 < 2 * bits:
            spread(2 * bits - 2 - step, p)

    def taps(a, b, ready):
        res = jnp.dot(xt[2 - a], gw[b], preferred_element_type=F32)
        for c in range(3):
            at = ((a * 3 + b) * 3 + c) * chans
            acc[at : at + chans, :] = res[:, c * ce : (c + 1) * ce]
        for p in ready:
            begin(p)

    def put_gown(k):
        live = t + k < T
        if k == 0:
            value = gs[...].astype(F32)
        else:
            take(later[k - 1], gh.at[k - 1], live)
            if k == 1:
                later.append(push(gh.at[0], gh.at[1], behind, live & has_before))
            value = jnp.where(live, gh[k - 1].astype(F32), 0.0)
        fbuf[1 : rows + 1, 0:cols, :] = value
        take(rims[k][0], ge_in.at[k, 0], live & (s > 0))
        take(rims[k][1], ge_in.at[k, 1], live & (s + 1 < S))
        left = jnp.where(live & (s > 0), ge_in[k, 0].astype(F32), 0.0)
        right = jnp.where(live & (s < S - 1), ge_in[k, 1].astype(F32), 0.0)
        for h in range(rows):
            fbuf[h, pitch - 1 : pitch, :] = left[h : h + 1]
            fbuf[h + 1, cols : cols + 1, :] = right[h : h + 1]
        f = fbuf[...].reshape(flat_all, chans)
        for c, w in enumerate((pltpu.roll(f, flat_all - 1, 0), f, pltpu.roll(f, 1, 0))):
            gown[k, :, c * chans : (c + 1) * chans] = w.astype(BF16)

    counted = [0]

    def input_grad(a, b):
        if counted[0] == 0:
            load.wait()
        total = None if counted[0] == 0 else tot[...]
        for c in range(3):
            term = lax.dot_general(
                gown[2 - a, (2 - b) * pitch : (2 - b) * pitch + flat, c * chans : (c + 1) * chans],
                wbuf[a, b, c], (((1,), (1,)), ((), ())), preferred_element_type=F32,
            )
            total = term if total is None else total + term
        counted[0] += 1
        if counted[0] < 9:
            tot[...] = total
        else:
            gi_ref[0] = total.reshape(rows, pitch, chans)[:, 0:cols, :].astype(BF16)

    for task in plan(bits, sizes, orders, starts, ce * 2):
        if task[0] == "taps":
            taps(*task[1:])
        elif task[0] == "arrive":
            arrive(*task[1:])
        elif task[0] == "gown":
            put_gown(task[1])
        else:
            input_grad(*task[1:])

    for copy in copies:
        copy.wait_send()
    for copy, ok in sent:
        if ok is None:
            copy.wait_send()
        else:
            pl.when(ok)(copy.wait_send)
    for which in range(2):
        pltpu.make_async_copy(st_in.at[which], st_in.at[which], st_send.at[which]).wait()


def solution(mesh):
    T, S = mesh.shape["tm"], mesh.shape["space"]

    def shards(conv_input, conv_out, kernel, gain, bias, cotangent):
        _, rows, cols, chans = conv_out.shape
        width = cols * S
        ce = chans // S
        bits = T.bit_length() - 1
        groups = round_up(27 * chans, T * 16) // (T * 16)
        streams = min(STREAMS, groups)
        sizes = [(groups // streams + (p < groups % streams)) * T * 16 for p in range(streams)]
        total_rows = sum(sizes)
        pitch = round_up(cols + 2, 16)
        depth = round_up(rows * width, 128)
        fx_rows = (depth + width - 1) // width
        fg_rows = max(rows + 2, (2 * width + depth + width - 1) // width)
        n_bulk = (S - 1) * 2 + 2 * S + 2 + 6
        vmem = pl.BlockSpec(memory_space=pltpu.VMEM)
        whole = pl.BlockSpec(memory_space=pl.ANY)
        gi, gk, gg, gb = pl.pallas_call(
            functools.partial(body, T, S, sizes),
            out_shape=(
                jax.ShapeDtypeStruct(conv_input.shape, BF16),
                jax.ShapeDtypeStruct((total_rows, ce), BF16),
                jax.ShapeDtypeStruct((1, chans), F32),
                jax.ShapeDtypeStruct((1, chans), F32),
            ),
            in_specs=[whole, whole, whole, vmem, vmem, whole],
            out_specs=(vmem, vmem, vmem, vmem),
            scratch_shapes=[
                pltpu.VMEM((3, S, rows, cols, chans), BF16),
                pltpu.VMEM(conv_out.shape, BF16),
                pltpu.VMEM(cotangent.shape, BF16),
                pltpu.VMEM((S, 2, rows, cols, ce), BF16),
                pltpu.VMEM((S, 2, rows, cols, ce), BF16),
                pltpu.VMEM((2, 2 * chans // 128, 128), F32),
                pltpu.VMEM((2, T * S - 1, 2 * chans // 128, 128), F32),
                pltpu.VMEM((2, rows, cols, chans), F32),
                pltpu.VMEM((S, 2, rows, cols, ce), F32),
                pltpu.VMEM((fx_rows, width, chans), F32),
                pltpu.VMEM((fg_rows, width, ce), F32),
                pltpu.VMEM((rows + 2, pitch, chans), F32),
                pltpu.VMEM((rows, cols, chans), BF16),
                pltpu.VMEM((2, rows, cols, chans), BF16),
                pltpu.VMEM((2, rows, chans), BF16),
                pltpu.VMEM((3, 2, rows, chans), BF16),
                pltpu.VMEM((3, (rows + 2) * pitch, 3 * chans), BF16),
                pltpu.VMEM((3, depth, 3 * ce), BF16),
                pltpu.VMEM((3, chans, depth), BF16),
                pltpu.VMEM((3, 3, 3, chans, chans), BF16),
                pltpu.VMEM((rows * pitch, chans), F32),
                pltpu.VMEM((total_rows, ce), F32),
                pltpu.VMEM((total_rows, ce), BF16),
                pltpu.VMEM((total_rows, ce), BF16),
                pltpu.SemaphoreType.DMA((4,)),
                pltpu.SemaphoreType.DMA,
                pltpu.SemaphoreType.DMA((2,)),
                pltpu.SemaphoreType.DMA((2,)),
                pltpu.SemaphoreType.DMA((n_bulk,)),
                pltpu.SemaphoreType.DMA((n_bulk,)),
                pltpu.SemaphoreType.DMA((2, streams, bits)),
                pltpu.SemaphoreType.DMA((2, streams, bits)),
            ],
            compiler_params=pltpu.CompilerParams(
                collective_id=0, has_side_effects=True, vmem_limit_bytes=60 * 1024 * 1024
            ),
        )(conv_input, conv_out, kernel, gain.reshape(1, chans), bias.reshape(1, chans), cotangent)
        part_rows = 27 * chans // PARTS
        gi, gk, gg, gb = pl.pallas_call(
            hand_out,
            grid=(PARTS,),
            out_shape=(
                jax.ShapeDtypeStruct(gi.shape, BF16),
                jax.ShapeDtypeStruct((27 * chans, ce), F32),
                jax.ShapeDtypeStruct((1, chans), F32),
                jax.ShapeDtypeStruct((1, chans), F32),
            ),
            in_specs=[
                pl.BlockSpec(gi.shape, lambda i: (0, 0, 0, 0)),
                pl.BlockSpec((part_rows, ce), lambda i: (i, 0)),
                pl.BlockSpec((1, chans), lambda i: (0, 0)),
                pl.BlockSpec((1, chans), lambda i: (0, 0)),
            ],
            out_specs=(
                pl.BlockSpec(gi.shape, lambda i: (0, 0, 0, 0)),
                pl.BlockSpec((part_rows, ce), lambda i: (i, 0)),
                pl.BlockSpec((1, chans), lambda i: (0, 0)),
                pl.BlockSpec((1, chans), lambda i: (0, 0)),
            ),
        )(gi, gk, gg, gb)
        return gi, gk.reshape(3, 3, 3, chans, ce), gg.reshape(chans), gb.reshape(chans)

    strip = P("tm", None, "space", None)
    return jax.shard_map(
        shards,
        mesh=mesh,
        in_specs=(strip, strip, P(), P(), P(), strip),
        out_specs=(strip, P(None, None, None, None, "space"), P(), P()),
        check_vma=False,
    )
```

time: 63 us -> 65 us (1.032); the launches traced: 61.8 us -> 64.8 us
  Pallas kernels: 61.1 us -> 64.1 us
    pallas_call x1, Pallas kernels: 58 us -> 60 us  [shards(): pl.pallas_call(functools.partial(body, T, S, sizes), out_shape=(jax.Shape...]
    pallas_call x1, Pallas kernels: 3.17 us -> 4.12 us  [shards(): pl.pallas_call(hand_out, grid=(PARTS,), out_shape=(jax.ShapeDtypeStruct(g...]
where the time goes in v1:
time: 65 us; the launch traced here: 64.8 us
  Pallas kernels  64.1 us (99%)
    pallas_call x1, Pallas kernels, shards(): pl.pallas_call(functools.partial(body, T, S, sizes), out_shape=(jax.Shape...  60 us
    pallas_call x1, Pallas kernels, shards(): pl.pallas_call(hand_out, grid=(PARTS,), out_shape=(jax.ShapeDtypeStruct(g...  4.12 us

profile of v1, /device:TPU:0, one launch (start us, length us, event | category | flops | bytes accessed | tf_op | source)
XLA Modules:
  0.0 64.8 jit_solution(13221364009646938199)
XLA Ops:
  0.6 60.0 %shard_map.93 = (bf16[1,12,20,256]{3,2,1,0:T(8,128)(2,1)}, bf16[6912,128]{1,0:T(8,128)(2,1)}, f32[1,256]{1,0:T(1,128)}, f32[1,256]{1,0:T(1,128)}) custom-call(bf16[1,12,20,256]{3,2,1,0:T(8,128)(2,1)} %x_hbm.1, bf16[1,12,20,256]{3,2,1,0:T(8,128)(2,1)} %co_hbm.1, bf16[3,3,3,256,256]{4,3,2,1,0:T(8,128)(2,1)} %k_hbm.1, f32[1,256]{1,0:T(1,128)} %bitcast.5, ...), custom_call_target="tpu_custom_call" | custom-call | tf_op jit(solution)/shard_map/pallas_call | solution.py:527
  60.6 4.1 %shard_map.94 = (bf16[1,12,20,256]{3,2,1,0:T(8,128)(2,1)}, f32[6912,128]{1,0:T(8,128)}, f32[1,256]{1,0:T(1,128)}, f32[1,256]{1,0:T(1,128)}) custom-call(bf16[1,12,20,256]{3,2,1,0:T(8,128)(2,1)} %get-tuple-element.12.gi_in, bf16[6912,128]{1,0:T(8,128)(2,1)} %get-tuple-element.13.gk_in, f32[1,256]{1,0:T(1,128)} %get-tuple-element.14.gg_in, ...), custom_call_target="tpu_custom_call" | custom-call | tf_op jit(solution)/shard_map/pallas_call | solution.py:576

commit v2 on v1

--- a/solution.py
+++ b/solution.py
@@ -9,8 +9,8 @@
 from jax.sharding import PartitionSpec as P
 
 GROUPS = 32
-STREAMS = 9
-PARTS = 4
+STREAMS = 13
+PARTS = 2
 EPSILON = 1e-06
 MESH = pl.DeviceIdType.MESH
 F32 = jnp.float32
@@ -46,8 +46,8 @@
 TAPS_A = (2, 1, 0)
 MATMUL = 0.36
 FILLER = 0.36
-ON_CHIP = (1.0, 250e3)
-ON_LINK = (1.7, 42e3)
+ON_CHIP = (1.1, 200e3)
+ON_LINK = (1.7, 46e3)
 FAR = 0.75
 
 
@@ -56,7 +56,7 @@
     swapped = list(range(bits))
     if bits > 2:
         swapped[1], swapped[2] = swapped[2], swapped[1]
-    return [swapped if p % 4 == 2 else straight for p in range(streams)]
+    return [swapped if p % 2 else straight for p in range(streams)]
 
 
 def stream_starts(sizes, chans):
@@ -94,8 +94,9 @@
         heapq.heappush(heap, (begin + time + latency, step, p))
 
     matmuls = list(starts)
-    fillers = [(0.0, ("gown", 0)), (4.5, ("gown", 1)), (7.5, ("gown", 2))]
-    fillers += [(0.0, ("input", a, b)) for a in TAPS_A for b in range(3)]
+    fillers = [(0.0, ("gown", 0))] + [(0.0, ("input", 2, b)) for b in range(3)]
+    fillers += [(7.0, ("gown", 1))] + [(0.0, ("input", 1, b)) for b in range(3)]
+    fillers += [(11.0, ("gown", 2))] + [(0.0, ("input", 0, b)) for b in range(3)]
     tasks, now = [], 0.0
     while heap or matmuls or fillers:
         if heap and heap[0][0] <= now:
@@ -110,13 +111,11 @@
             now += MATMUL
             for p in ready:
                 send(now, p, 0)
-        elif fillers and fillers[0][0] <= now:
+        elif fillers and fillers[0][0] <= now and (not heap or heap[0][0] - now >= 0.8 * FILLER):
             tasks.append(fillers.pop(0)[1])
             now += FILLER
         else:
-            times = [heap[0][0]] if heap else []
-            times += [fillers[0][0]] if fillers else []
-            now = min(times)
+            now = heap[0][0] if heap else fillers[0][0]
     return tasks
 
 
@@ -231,11 +230,11 @@
     behind = (frame(-1), s)
     has_next, has_before = t + 1 < T, t > 0
     cut, mate, past = [], [], [[], []]
-    for r in range(1, S):
-        cut.append(push(slice_out.at[strip(-r)], cw.at[s], (t, strip(-r))))
     past[0].append(push(xw.at[0, s], xw.at[1, s], ahead, has_next))
     for r in range(1, S):
         mate.append(push(xw.at[0, s], xw.at[0, s], (t, strip(-r))))
+    for r in range(1, S):
+        cut.append(push(slice_out.at[strip(-r)], cw.at[s], (t, strip(-r))))
 
     def relay(k, r):
         j = strip(r)
@@ -259,8 +258,6 @@
     group = chans // GROUPS
     count = rows * width * T * group
     relay(1, 0)
-    for r in range(1, S):
-        relay(0, r)
     sums = take_stats(0)
     grouped = group_sum(sums, group)
     mean2 = grouped[:halves] / count
@@ -294,7 +291,8 @@
         return out
 
     for r in range(1, S):
-        relay(1, r)
+        relay(0, r)
+    for r in range(1, S):
         take(cut[r - 1], cw.at[strip(r)])
     keep.wait()
     firsts = tuple(part(p) for p in (mean, inv, gain, bias))
@@ -313,11 +311,9 @@
         xt[k] = jnp.transpose(placed).astype(BF16)
 
     put_input(0)
+    for r in range(1, S):
+        relay(1, r)
     put_input(1)
-    relay_second = t > 1
-    for r in range(S):
-        take(past[1][r], xw.at[2, strip(r)], relay_second)
-    put_input(2)
     sums = take_stats(1)
     chan_bias, chan_gain = wide(sums[:halves]), wide(sums[halves:])
     gb_ref[...] = chan_bias
@@ -334,7 +330,11 @@
     for h in range(rows):
         ge_out[0, h : h + 1, :] = g[h, 0:1, :].astype(BF16)
         ge_out[1, h : h + 1, :] = g[h, cols - 1 : cols, :].astype(BF16)
-    later = [push(gs, gh.at[0], behind, has_before)]
+    odd = lax.rem(t, 2) == 1
+    later = [
+        push(gs, gh.at[0], behind, has_before),
+        push(gs, gh.at[1], (frame(-2), s), odd & (t > 1)),
+    ]
     rims = []
     for k in range(3):
         back = (frame(-k), strip(1)), (frame(-k), strip(-1))
@@ -438,6 +438,10 @@
             spread(2 * bits - 2 - step, p)
 
     def taps(a, b, ready):
+        if a == TAPS_A[-1] and b == 0:
+            for r in range(S):
+                take(past[1][r], xw.at[2, strip(r)], t > 1)
+            put_input(2)
         res = jnp.dot(xt[2 - a], gw[b], preferred_element_type=F32)
         for c in range(3):
             at = ((a * 3 + b) * 3 + c) * chans
@@ -450,9 +454,12 @@
         if k == 0:
             value = gs[...].astype(F32)
         else:
-            take(later[k - 1], gh.at[k - 1], live)
             if k == 1:
-                later.append(push(gh.at[0], gh.at[1], behind, live & has_before))
+                take(later[0], gh.at[0], live)
+                later.append(push(gh.at[0], gh.at[1], behind, live & odd))
+            else:
+                take(later[1], gh.at[1], live & odd)
+                take(later[2], gh.at[1], live & (lax.rem(t, 2) == 0))
             value = jnp.where(live, gh[k - 1].astype(F32), 0.0)
         fbuf[1 : rows + 1, 0:cols, :] = value
         take(rims[k][0], ge_in.at[k, 0], live & (s > 0))
@@ -521,7 +528,7 @@
         depth = round_up(rows * width, 128)
         fx_rows = (depth + width - 1) // width
         fg_rows = max(rows + 2, (2 * width + depth + width - 1) // width)
-        n_bulk = (S - 1) * 2 + 2 * S + 2 + 6
+        n_bulk = (S - 1) * 2 + 2 * S + 3 + 6
         vmem = pl.BlockSpec(memory_space=pltpu.VMEM)
         whole = pl.BlockSpec(memory_space=pl.ANY)
         gi, gk, gg, gb = pl.pallas_call(

time: 65 us -> 59.6 us (0.917)
  Pallas kernels: 64.1 us -> 58.4 us
    pallas_call x1, Pallas kernels: 60 us -> 55.3 us  [shards(): pl.pallas_call(functools.partial(body, T, S, sizes), out_shape=(jax.Shape...]
    pallas_call x1, Pallas kernels: 4.12 us -> 3.17 us  [shards(): pl.pallas_call(hand_out, grid=(PARTS,), out_shape=(jax.ShapeDtypeStruct(g...]
where the time goes in v2:
time: 59.6 us; the launch traced here: 59.1 us
  Pallas kernels  58.4 us (98%)
  between operations  0.64 us (1%)
    pallas_call x1, Pallas kernels, shards(): pl.pallas_call(functools.partial(body, T, S, sizes), out_shape=(jax.Shape...  55.3 us
    pallas_call x1, Pallas kernels, shards(): pl.pallas_call(hand_out, grid=(PARTS,), out_shape=(jax.ShapeDtypeStruct(g...  3.17 us

profile of v2, /device:TPU:0, one launch (start us, length us, event | category | flops | bytes accessed | tf_op | source)
XLA Modules:
  0.0 59.1 jit_solution(1818013691188882700)
XLA Ops:
  0.6 55.3 %shard_map.93 = (bf16[1,12,20,256]{3,2,1,0:T(8,128)(2,1)}, bf16[6912,128]{1,0:T(8,128)(2,1)}, f32[1,256]{1,0:T(1,128)}, f32[1,256]{1,0:T(1,128)}) custom-call(bf16[1,12,20,256]{3,2,1,0:T(8,128)(2,1)} %x_hbm.1, bf16[1,12,20,256]{3,2,1,0:T(8,128)(2,1)} %co_hbm.1, bf16[3,3,3,256,256]{4,3,2,1,0:T(8,128)(2,1)} %k_hbm.1, f32[1,256]{1,0:T(1,128)} %bitcast.5, ...), custom_call_target="tpu_custom_call" | custom-call | tf_op jit(solution)/shard_map/pallas_call | solution.py:534
  55.9 3.2 %shard_map.94 = (bf16[1,12,20,256]{3,2,1,0:T(8,128)(2,1)}, f32[6912,128]{1,0:T(8,128)}, f32[1,256]{1,0:T(1,128)}, f32[1,256]{1,0:T(1,128)}) custom-call(bf16[1,12,20,256]{3,2,1,0:T(8,128)(2,1)} %get-tuple-element.12.gi_in, bf16[6912,128]{1,0:T(8,128)(2,1)} %get-tuple-element.13.gk_in, f32[1,256]{1,0:T(1,128)} %get-tuple-element.14.gg_in, ...), custom_call_target="tpu_custom_call" | custom-call | tf_op jit(solution)/shard_map/pallas_call | solution.py:583

commit v3 on v2

--- a/solution.py
+++ b/solution.py
@@ -119,13 +119,36 @@
     return tasks
 
 
+EVENTS = ((1.06, 0.31), (3.7, 0.72), (5.7, 0.73), (7.69, 0.73), (9.53, 0.71), (11.68, 0.76), (13.94, 1.05))
+FILL_AT = (4.45, 12.45, 17.5)
+FILL_STEP = 1.09
+LINE = 4
+
+
+def tree_plan(starts, streams):
+    tasks, number = [], 0
+    for i, ((a, b), ready) in enumerate(starts):
+        tasks.append((i * MATMUL, ("taps", a, b, ready)))
+        for p in ready:
+            last = i * MATMUL
+            for e, (first, step) in enumerate(EVENTS):
+                last = max(last + 1e-3, first + step * number * 13 / streams)
+                tasks.append((last, ("tree", p, e)))
+            number += 1
+    for k, a in enumerate(TAPS_A):
+        tasks.append((FILL_AT[k], ("gown", k)))
+        for b in range(3):
+            tasks.append((FILL_AT[k] + (b + 1) * FILL_STEP, ("input", a, b)))
+    return [task for _, task in sorted(tasks, key=lambda item: item[0])]
+
+
 def body(
     T, S, sizes,
     x_hbm, co_hbm, k_hbm, gain_ref, bias_ref, ct_hbm,
     gi_ref, gk_ref, gg_ref, gb_ref,
     xw, co_ref, ct_ref, slice_out, cw, st_out, st_in, own, pre, fx, fg, fbuf,
-    gs, gh, ge_out, ge_in, gown, gw, xt, wbuf, tot, acc, sbuf, rbuf,
-    in_sem, w_sem, st_send, st_recv, bulk_send, bulk_recv, rs_send, rs_recv,
+    gs, gh, ge_out, ge_in, gown, gw, xt, wbuf, tot, acc, sbuf, rbuf, zbuf,
+    in_sem, w_sem, st_send, st_recv, bulk_send, bulk_recv, rs_send, rs_recv, tree_send, tree_recv,
 ):
     N = T * S
     total_rows = sum(sizes)
@@ -200,7 +223,7 @@
 
     sent = []
 
-    def push(src, dst, device, ok=None):
+    def push(src, dst, device, ok=None, now=None):
         i = len(sent)
         copy = pltpu.make_async_remote_copy(
             src_ref=src, dst_ref=dst, send_sem=bulk_send.at[i], recv_sem=bulk_recv.at[i],
@@ -209,7 +232,7 @@
         if ok is None:
             copy.start()
         else:
-            pl.when(ok)(copy.start)
+            pl.when(ok if now is None else now)(copy.start)
         sent.append((copy, ok))
         return i
 
@@ -236,16 +259,20 @@
     for r in range(1, S):
         cut.append(push(slice_out.at[strip(-r)], cw.at[s], (t, strip(-r))))
 
-    def relay(k, r):
-        j = strip(r)
-        if k == 0:
-            take(mate[r - 1], xw.at[0, j])
-            ok = has_next
-        else:
-            take(past[k - 1][r], xw.at[k, j], has_before)
-            ok = has_next & has_before
-        if k < 2:
-            past[k].append(push(xw.at[k, j], xw.at[k + 1, j], ahead, ok))
+    odd = lax.rem(t, 2) == 1
+    even = lax.rem(t, 2) == 0
+
+    def relay_near(r):
+        take(mate[r - 1], xw.at[0, strip(r)])
+        past[0].append(push(xw.at[0, strip(r)], xw.at[1, strip(r)], ahead, has_next))
+
+    def relay_far(r, when):
+        take(past[0][r], xw.at[1, strip(r)], has_before & when)
+        ok = has_next & has_before
+        if r < len(past[1]):
+            pl.when(ok & when)(sent[past[1][r]][0].start)
+        else:
+            past[1].append(push(xw.at[1, strip(r)], xw.at[2, strip(r)], ahead, ok, ok & when))
 
     fx[...] = jnp.zeros_like(fx)
     fg[...] = jnp.zeros_like(fg)
@@ -257,7 +284,8 @@
     bias = bias_ref[...]
     group = chans // GROUPS
     count = rows * width * T * group
-    relay(1, 0)
+    relay_far(0, odd)
+    relay_far(0, even)
     sums = take_stats(0)
     grouped = group_sum(sums, group)
     mean2 = grouped[:halves] / count
@@ -291,7 +319,9 @@
         return out
 
     for r in range(1, S):
-        relay(0, r)
+        relay_near(r)
+    for r in range(1, S):
+        relay_far(r, odd)
     for r in range(1, S):
         take(cut[r - 1], cw.at[strip(r)])
     keep.wait()
@@ -312,7 +342,7 @@
 
     put_input(0)
     for r in range(1, S):
-        relay(1, r)
+        relay_far(r, even)
     put_input(1)
     sums = take_stats(1)
     chan_bias, chan_gain = wide(sums[:halves]), wide(sums[halves:])
@@ -330,7 +360,6 @@
     for h in range(rows):
         ge_out[0, h : h + 1, :] = g[h, 0:1, :].astype(BF16)
         ge_out[1, h : h + 1, :] = g[h, cols - 1 : cols, :].astype(BF16)
-    odd = lax.rem(t, 2) == 1
     later = [
         push(gs, gh.at[0], behind, has_before),
         push(gs, gh.at[1], (frame(-2), s), odd & (t > 1)),
@@ -391,11 +420,132 @@
         copies.append(copy)
         flying[p] = copy
 
+    tree = T == 4 * LINE
+    z, x, core = t // 4, lax.rem(t // 2, 2), lax.rem(t, 2)
+    side_z = z // 2
+    inner = (z == 1) | (z == 2)
+    outer = (z == 0) | (z == 3)
+    toward = jnp.where(inner, z - 1 + 2 * side_z, z + 1 - 2 * side_z)
+    mates = {
+        "core": (t + 1 - 2 * core, s),
+        "x": (t + 2 - 4 * x, s),
+        "line": (toward * 4 + lax.rem(t, 4), s),
+        "middle": (lax.rem(3 - z + T, T) * 4 + lax.rem(t, 4), s),
+    }
+    slots = {"c0": 0, "x0": 1, "z0": 2, "z1": 3, "a2b": 3, "a1": 4, "a2a": 4, "x1": 5}
+
+    def tree_push(p, kind, src, dst, device):
+        by_role = kind in ("z0", "z1", "a1", "a2a", "a2b")
+        pltpu.make_async_remote_copy(
+            src_ref=src, dst_ref=dst, send_sem=tree_send.at[int(by_role)],
+            recv_sem=tree_send.at[2] if kind == "c1" else tree_recv.at[p, slots[kind]],
+            device_id=device, device_id_type=MESH,
+        ).start()
+
+    def tree_wait(p, kind, ref):
+        pltpu.make_async_copy(ref, ref, tree_recv.at[p, slots[kind]]).wait()
+
+    def places(p):
+        half, n, h = sizes[p] // 2, sizes[p] // 4, sizes[p] // 8
+        mine = core * half + x * n
+        apart = core * half + (1 - x) * n
+        return half, n, h, mine, apart
+
+    def rows_of(ref, p, off, n):
+        return ref.at[span(p, off, n)]
+
+    def tree_event(p, e):
+        half, n, h, mine, apart = places(p)
+        base = bases[p]
+        near, far = mine + side_z * h, mine + (1 - side_z) * h
+        at_x, at_z = half, half + n
+        zrow = pl.ds(base // 8, h)
+
+        def taken(ref, off, rows):
+            return ref[span(p, off, rows), :]
+
+        def put_half(kind, off, device):
+            tree_push(p, kind, rows_of(gk_ref, p, off, h), rows_of(gk_ref, p, off, h), device)
+
+        def put_whole(kind, off):
+            tree_push(p, kind, rows_of(gk_ref, p, off, n), rows_of(gk_ref, p, off, n), mates["core"])
+
+        if e == 0:
+            tree_wait(p, "c0", rows_of(rbuf, p, 0, half))
+            value = taken(acc, apart, n) + taken(rbuf, (1 - x) * n, n).astype(F32)
+            sbuf[span(p, at_x, n), :] = value.astype(BF16)
+            tree_push(p, "x0", rows_of(sbuf, p, at_x, n), rows_of(rbuf, p, at_x, n), mates["x"])
+            acc[span(p, mine, n), :] = taken(acc, mine, n) + taken(rbuf, x * n, n).astype(F32)
+        elif e == 1:
+            tree_wait(p, "x0", rows_of(rbuf, p, at_x, n))
+
+            @pl.when(outer)
+            def _():
+                value = taken(acc, mine, n) + taken(rbuf, at_x, n).astype(F32)
+                sbuf[span(p, at_z, n), :] = value.astype(BF16)
+                tree_push(p, "z0", rows_of(sbuf, p, at_z, n), rows_of(rbuf, p, at_z, n), mates["line"])
+
+            @pl.when(inner)
+            def _():
+                acc[span(p, mine, n), :] = taken(acc, mine, n) + taken(rbuf, at_x, n).astype(F32)
+        elif e == 2:
+            @pl.when(inner)
+            def _():
+                tree_wait(p, "z0", rows_of(rbuf, p, at_z, n))
+                value = taken(acc, far, h) + taken(rbuf, at_z + (1 - side_z) * h, h).astype(F32)
+                sbuf[span(p, at_z, h), :] = value.astype(BF16)
+                tree_push(p, "z1", rows_of(sbuf, p, at_z, h), zbuf.at[zrow], mates["middle"])
+                acc[span(p, near, h), :] = taken(acc, near, h) + taken(rbuf, at_z + side_z * h, h).astype(F32)
+        elif e == 3:
+            @pl.when(inner)
+            def _():
+                tree_wait(p, "z1", zbuf.at[zrow])
+                gk_ref[span(p, near, h), :] = (taken(acc, near, h) + zbuf[zrow, :].astype(F32)).astype(BF16)
+                put_half("x1", near, mates["x"])
+                put_half("a1", near, mates["middle"])
+                put_half("a2a", near, mates["line"])
+        elif e == 4:
+            @pl.when(inner)
+            def _():
+                tree_wait(p, "a1", rows_of(gk_ref, p, far, h))
+                put_half("x1", far, mates["x"])
+                put_half("a2b", far, mates["line"])
+                put_whole("c1", mine)
+
+            @pl.when(outer)
+            def _():
+                tree_wait(p, "a2a", rows_of(gk_ref, p, near, h))
+                put_half("x1", near, mates["x"])
+        elif e == 5:
+            @pl.when(outer)
+            def _():
+                tree_wait(p, "a2b", rows_of(gk_ref, p, far, h))
+                put_half("x1", far, mates["x"])
+                put_whole("c1", mine)
+        else:
+            tree_wait(p, "x1", rows_of(gk_ref, p, apart, n))
+            put_whole("c1", apart)
+
+    def tree_end():
+        for ref, i in ((gk_ref.at[0 : total_rows // 2], 2), (acc.at[0 : total_rows * 3 // 4], 0)):
+            pltpu.make_async_copy(ref, ref, tree_send.at[i]).wait()
+
+        @pl.when(outer)
+        def _():
+            pltpu.make_async_copy(sbuf.at[0 : total_rows // 4], sbuf.at[0 : total_rows // 4], tree_send.at[1]).wait()
+
+        @pl.when(inner)
+        def _():
+            pltpu.make_async_copy(sbuf.at[0 : total_rows // 2], sbuf.at[0 : total_rows // 2], tree_send.at[1]).wait()
+
     def begin(p):
         half = sizes[p] >> 1
         mine = side(orders[p][0])
         start = start_of(p, 0)
         sbuf[start : start + half, :] = acc[span(p, (1 - mine) * half, half), :].astype(BF16)
+        if tree:
+            tree_push(p, "c0", sbuf.at[start : start + half], rbuf.at[start : start + half], mates["core"])
+            return
         launch(0, p)
         offs[p] = mine * half
 
@@ -491,15 +641,20 @@
         else:
             gi_ref[0] = total.reshape(rows, pitch, chans)[:, 0:cols, :].astype(BF16)
 
-    for task in plan(bits, sizes, orders, starts, ce * 2):
+    tasks = tree_plan(starts, streams) if tree else plan(bits, sizes, orders, starts, ce * 2)
+    for task in tasks:
         if task[0] == "taps":
             taps(*task[1:])
         elif task[0] == "arrive":
             arrive(*task[1:])
+        elif task[0] == "tree":
+            tree_event(*task[1:])
         elif task[0] == "gown":
             put_gown(task[1])
         else:
             input_grad(*task[1:])
+    if tree:
+        tree_end()
 
     for copy in copies:
         copy.wait_send()
@@ -529,6 +684,8 @@
         fx_rows = (depth + width - 1) // width
         fg_rows = max(rows + 2, (2 * width + depth + width - 1) // width)
         n_bulk = (S - 1) * 2 + 2 * S + 3 + 6
+        tree = T == 4 * LINE
+        halving, line = ((1, 1, 1), (streams, 6)) if tree else ((2, streams, bits), (1, 1))
         vmem = pl.BlockSpec(memory_space=pltpu.VMEM)
         whole = pl.BlockSpec(memory_space=pl.ANY)
         gi, gk, gg, gb = pl.pallas_call(
@@ -566,14 +723,17 @@
                 pltpu.VMEM((total_rows, ce), F32),
                 pltpu.VMEM((total_rows, ce), BF16),
                 pltpu.VMEM((total_rows, ce), BF16),
+                pltpu.VMEM((total_rows // 8, ce), BF16),
                 pltpu.SemaphoreType.DMA((4,)),
                 pltpu.SemaphoreType.DMA,
                 pltpu.SemaphoreType.DMA((2,)),
                 pltpu.SemaphoreType.DMA((2,)),
                 pltpu.SemaphoreType.DMA((n_bulk,)),
                 pltpu.SemaphoreType.DMA((n_bulk,)),
-                pltpu.SemaphoreType.DMA((2, streams, bits)),
-                pltpu.SemaphoreType.DMA((2, streams, bits)),
+                pltpu.SemaphoreType.DMA(halving),
+                pltpu.SemaphoreType.DMA(halving),
+                pltpu.SemaphoreType.DMA((3,)),
+                pltpu.SemaphoreType.DMA(line),
             ],
             compiler_params=pltpu.CompilerParams(
                 collective_id=0, has_side_effects=True, vmem_limit_bytes=60 * 1024 * 1024

time: 59.6 us -> 58.4 us (0.980)
  Pallas kernels: 58.4 us -> 57.6 us
    pallas_call x1, Pallas kernels: 55.3 us -> 54.4 us  [shards(): pl.pallas_call(functools.partial(body, T, S, sizes), out_shape=(jax.Shape...]
where the time goes in v3:
time: 58.4 us; the launch traced here: 58.2 us
  Pallas kernels  57.6 us (99%)
  between operations  0.64 us (1%)
    pallas_call x1, Pallas kernels, shards(): pl.pallas_call(functools.partial(body, T, S, sizes), out_shape=(jax.Shape...  54.4 us
    pallas_call x1, Pallas kernels, shards(): pl.pallas_call(hand_out, grid=(PARTS,), out_shape=(jax.ShapeDtypeStruct(g...  3.17 us

profile of v3, /device:TPU:0, one launch (start us, length us, event | category | flops | bytes accessed | tf_op | source)
XLA Modules:
  0.0 58.2 jit_solution(10108407896879559687)
XLA Ops:
  0.6 54.4 %shard_map.93 = (bf16[1,12,20,256]{3,2,1,0:T(8,128)(2,1)}, bf16[6912,128]{1,0:T(8,128)(2,1)}, f32[1,256]{1,0:T(1,128)}, f32[1,256]{1,0:T(1,128)}) custom-call(bf16[1,12,20,256]{3,2,1,0:T(8,128)(2,1)} %x_hbm.1, bf16[1,12,20,256]{3,2,1,0:T(8,128)(2,1)} %co_hbm.1, bf16[3,3,3,256,256]{4,3,2,1,0:T(8,128)(2,1)} %k_hbm.1, f32[1,256]{1,0:T(1,128)} %bitcast.5, ...), custom_call_target="tpu_custom_call" | custom-call | tf_op jit(solution)/shard_map/pallas_call | solution.py:691
  55.0 3.2 %shard_map.94 = (bf16[1,12,20,256]{3,2,1,0:T(8,128)(2,1)}, f32[6912,128]{1,0:T(8,128)}, f32[1,256]{1,0:T(1,128)}, f32[1,256]{1,0:T(1,128)}) custom-call(bf16[1,12,20,256]{3,2,1,0:T(8,128)(2,1)} %get-tuple-element.12.gi_in, bf16[6912,128]{1,0:T(8,128)(2,1)} %get-tuple-element.13.gk_in, f32[1,256]{1,0:T(1,128)} %get-tuple-element.14.gg_in, ...), custom_call_target="tpu_custom_call" | custom-call | tf_op jit(solution)/shard_map/pallas_call | solution.py:743

commit v4 on v3

--- a/solution.py
+++ b/solution.py
@@ -10,7 +10,7 @@
 
 GROUPS = 32
 STREAMS = 13
-PARTS = 2
+PARTS = 3
 EPSILON = 1e-06
 MESH = pl.DeviceIdType.MESH
 F32 = jnp.float32
@@ -33,14 +33,19 @@
     return x
 
 
-def hand_out(gi_in, gk_in, gg_in, gb_in, gi_out, gk_out, gg_out, gb_out):
-    gk_out[...] = gk_in[...].astype(F32)
-
-    @pl.when(pl.program_id(0) == 0)
-    def _():
-        gi_out[...] = gi_in[...]
-        gg_out[...] = gg_in[...]
-        gb_out[...] = gb_in[...]
+def hand_out(gi_in, gk_in, gg_in, gb_in, gi_out, gk_out, gg_out, gb_out, wide, sems):
+    rows = gk_out.shape[0] // PARTS
+    copies = [pltpu.make_async_copy(gi_in, gi_out, sems.at[PARTS])]
+    copies[0].start()
+    for i in range(PARTS):
+        at = slice(i * rows, (i + 1) * rows)
+        wide[at, :] = gk_in[at, :].astype(F32)
+        copies.append(pltpu.make_async_copy(wide.at[at], gk_out.at[at], sems.at[i]))
+        copies[-1].start()
+    gg_out[...] = gg_in[...]
+    gb_out[...] = gb_in[...]
+    for copy in copies:
+        copy.wait()
 
 
 TAPS_A = (2, 1, 0)
@@ -147,7 +152,7 @@
     x_hbm, co_hbm, k_hbm, gain_ref, bias_ref, ct_hbm,
     gi_ref, gk_ref, gg_ref, gb_ref,
     xw, co_ref, ct_ref, slice_out, cw, st_out, st_in, own, pre, fx, fg, fbuf,
-    gs, gh, ge_out, ge_in, gown, gw, xt, wbuf, tot, acc, sbuf, rbuf, zbuf,
+    gflat, gs, gr, gh, ge_out, ge_in, gown, gw, xt, wbuf, tot, acc, sbuf, rbuf, zbuf,
     in_sem, w_sem, st_send, st_recv, bulk_send, bulk_recv, rs_send, rs_recv, tree_send, tree_recv,
 ):
     N = T * S
@@ -356,14 +361,18 @@
         return inv * (grad * gain - plain - normed * product)
 
     g = conv_grad(own[0], own[1], inv, gain, plain, product)
-    gs[...] = g.astype(BF16)
+    for h in range(rows):
+        gflat[h * cols : (h + 1) * cols, :] = g[h]
+    gs[...] = gflat[...].astype(BF16)
     for h in range(rows):
         ge_out[0, h : h + 1, :] = g[h, 0:1, :].astype(BF16)
         ge_out[1, h : h + 1, :] = g[h, cols - 1 : cols, :].astype(BF16)
-    later = [
-        push(gs, gh.at[0], behind, has_before),
-        push(gs, gh.at[1], (frame(-2), s), odd & (t > 1)),
-    ]
+    second = (frame(-2), s)
+    later = {
+        "pair": push(gs, gr, ahead, even),
+        "near": push(gs, gh.at[0], behind, odd),
+        "far": push(gs, gh.at[1], second, odd & (t > 1)),
+    }
     rims = []
     for k in range(3):
         back = (frame(-k), strip(1)), (frame(-k), strip(-1))
@@ -598,6 +607,9 @@
             acc[at : at + chans, :] = res[:, c * ce : (c + 1) * ce]
         for p in ready:
             begin(p)
+        if (a, b) == (TAPS_A[0], 2):
+            take(later["pair"], gr, odd)
+            later["next"] = push(gr, gh.at[0], second, odd & (t > 1))
 
     def put_gown(k):
         live = t + k < T
@@ -605,13 +617,15 @@
             value = gs[...].astype(F32)
         else:
             if k == 1:
-                take(later[0], gh.at[0], live)
-                later.append(push(gh.at[0], gh.at[1], behind, live & odd))
+                take(later["near"], gh.at[0], live & even)
+                take(later["next"], gh.at[0], live & odd)
+                later["last"] = push(gh.at[0], gh.at[1], behind, live & odd)
             else:
-                take(later[1], gh.at[1], live & odd)
-                take(later[2], gh.at[1], live & (lax.rem(t, 2) == 0))
+                take(later["far"], gh.at[1], live & odd)
+                take(later["last"], gh.at[1], live & even)
             value = jnp.where(live, gh[k - 1].astype(F32), 0.0)
-        fbuf[1 : rows + 1, 0:cols, :] = value
+        for h in range(rows):
+            fbuf[h + 1, 0:cols, :] = value[h * cols : (h + 1) * cols]
         take(rims[k][0], ge_in.at[k, 0], live & (s > 0))
         take(rims[k][1], ge_in.at[k, 1], live & (s + 1 < S))
         left = jnp.where(live & (s > 0), ge_in[k, 0].astype(F32), 0.0)
@@ -683,20 +697,20 @@
         depth = round_up(rows * width, 128)
         fx_rows = (depth + width - 1) // width
         fg_rows = max(rows + 2, (2 * width + depth + width - 1) // width)
-        n_bulk = (S - 1) * 2 + 2 * S + 3 + 6
+        n_bulk = (S - 1) * 2 + 2 * S + 5 + 6
         tree = T == 4 * LINE
         halving, line = ((1, 1, 1), (streams, 6)) if tree else ((2, streams, bits), (1, 1))
         vmem = pl.BlockSpec(memory_space=pltpu.VMEM)
-        whole = pl.BlockSpec(memory_space=pl.ANY)
+        hbm = pl.BlockSpec(memory_space=pltpu.HBM)
         gi, gk, gg, gb = pl.pallas_call(
             functools.partial(body, T, S, sizes),
             out_shape=(
-                jax.ShapeDtypeStruct(conv_input.shape, BF16),
-                jax.ShapeDtypeStruct((total_rows, ce), BF16),
-                jax.ShapeDtypeStruct((1, chans), F32),
-                jax.ShapeDtypeStruct((1, chans), F32),
+                pltpu.VMEM(conv_input.shape, BF16),
+                pltpu.VMEM((total_rows, ce), BF16),
+                pltpu.VMEM((1, chans), F32),
+                pltpu.VMEM((1, chans), F32),
             ),
-            in_specs=[whole, whole, whole, vmem, vmem, whole],
+            in_specs=[hbm, hbm, hbm, vmem, vmem, hbm],
             out_specs=(vmem, vmem, vmem, vmem),
             scratch_shapes=[
                 pltpu.VMEM((3, S, rows, cols, chans), BF16),
@@ -711,8 +725,10 @@
                 pltpu.VMEM((fx_rows, width, chans), F32),
                 pltpu.VMEM((fg_rows, width, ce), F32),
                 pltpu.VMEM((rows + 2, pitch, chans), F32),
-                pltpu.VMEM((rows, cols, chans), BF16),
-                pltpu.VMEM((2, rows, cols, chans), BF16),
+                pltpu.VMEM((rows * cols, chans), F32),
+                pltpu.VMEM((rows * cols, chans), BF16),
+                pltpu.VMEM((rows * cols, chans), BF16),
+                pltpu.VMEM((2, rows * cols, chans), BF16),
                 pltpu.VMEM((2, rows, chans), BF16),
                 pltpu.VMEM((3, 2, rows, chans), BF16),
                 pltpu.VMEM((3, (rows + 2) * pitch, 3 * chans), BF16),
@@ -739,28 +755,18 @@
                 collective_id=0, has_side_effects=True, vmem_limit_bytes=60 * 1024 * 1024
             ),
         )(conv_input, conv_out, kernel, gain.reshape(1, chans), bias.reshape(1, chans), cotangent)
-        part_rows = 27 * chans // PARTS
         gi, gk, gg, gb = pl.pallas_call(
             hand_out,
-            grid=(PARTS,),
             out_shape=(
                 jax.ShapeDtypeStruct(gi.shape, BF16),
                 jax.ShapeDtypeStruct((27 * chans, ce), F32),
                 jax.ShapeDtypeStruct((1, chans), F32),
                 jax.ShapeDtypeStruct((1, chans), F32),
             ),
-            in_specs=[
-                pl.BlockSpec(gi.shape, lambda i: (0, 0, 0, 0)),
-                pl.BlockSpec((part_rows, ce), lambda i: (i, 0)),
-                pl.BlockSpec((1, chans), lambda i: (0, 0)),
-                pl.BlockSpec((1, chans), lambda i: (0, 0)),
-            ],
-            out_specs=(
-                pl.BlockSpec(gi.shape, lambda i: (0, 0, 0, 0)),
-                pl.BlockSpec((part_rows, ce), lambda i: (i, 0)),
-                pl.BlockSpec((1, chans), lambda i: (0, 0)),
-                pl.BlockSpec((1, chans), lambda i: (0, 0)),
-            ),
+            in_specs=[vmem, vmem, vmem, vmem],
+            out_specs=(hbm, hbm, vmem, vmem),
+            scratch_shapes=[pltpu.VMEM((27 * chans, ce), F32), pltpu.SemaphoreType.DMA((PARTS + 1,))],
+            compiler_params=pltpu.CompilerParams(vmem_limit_bytes=16 * 1024 * 1024),
         )(gi, gk, gg, gb)
         return gi, gk.reshape(3, 3, 3, chans, ce), gg.reshape(chans), gb.reshape(chans)
 

time: 58.4 us -> 55.9 us (0.957)
  Pallas kernels: 57.6 us -> 55.1 us
    pallas_call x2, Pallas kernels: 57.6 us -> 55.1 us  [the longest x1 52.7 us: shards(): pl.pallas_call(functools.partial(body, T, S, sizes), out_shape=(pltpu.VME...]
where the time goes in v4:
time: 55.9 us; the launch traced here: 55.8 us
  Pallas kernels  55.1 us (99%)
  between operations  0.64 us (1%)
    pallas_call x1, Pallas kernels, shards(): pl.pallas_call(functools.partial(body, T, S, sizes), out_shape=(pltpu.VME...  52.7 us
    pallas_call x1, Pallas kernels, shards(): pl.pallas_call(hand_out, out_shape=(jax.ShapeDtypeStruct(gi.shape, BF16),...  2.47 us

profile of v4, /device:TPU:0, one launch (start us, length us, event | category | flops | bytes accessed | tf_op | source)
XLA Modules:
  0.0 55.8 jit_solution(1816084337433264438)
XLA Ops:
  0.6 52.7 %shard_map.93 = (bf16[1,12,20,256]{3,2,1,0:T(8,128)(2,1)S(1)}, bf16[6912,128]{1,0:T(8,128)(2,1)S(1)}, f32[1,256]{1,0:T(1,128)S(1)}, f32[1,256]{1,0:T(1,128)S(1)}) custom-call(bf16[1,12,20,256]{3,2,1,0:T(8,128)(2,1)} %x_hbm.1, bf16[1,12,20,256]{3,2,1,0:T(8,128)(2,1)} %co_hbm.1, bf16[3,3,3,256,256]{4,3,2,1,0:T(8,128)(2,1)} %k_hbm.1, f32[1,256]{1,0:T(1,128)} %bitcast.5, ...), custom_call_target="tpu_custom_call" | custom-call | tf_op jit(solution)/shard_map/pallas_call | solution.py:705
  53.3 2.5 %shard_map.94 = (bf16[1,12,20,256]{3,2,1,0:T(8,128)(2,1)}, f32[6912,128]{1,0:T(8,128)}, f32[1,256]{1,0:T(1,128)}, f32[1,256]{1,0:T(1,128)}) custom-call(bf16[1,12,20,256]{3,2,1,0:T(8,128)(2,1)S(1)} %get-tuple-element.12.gi_in, bf16[6912,128]{1,0:T(8,128)(2,1)S(1)} %get-tuple-element.13.gk_in, f32[1,256]{1,0:T(1,128)S(1)} %get-tuple-element.14.gg_in, ...), custom_call_target="tpu_custom_call" | custom-call | tf_op jit(solution)/shard_map/pallas_call | solution.py:758

commit v5 on v4

--- a/solution.py
+++ b/solution.py
@@ -124,9 +124,9 @@
     return tasks
 
 
-EVENTS = ((1.06, 0.31), (3.7, 0.72), (5.7, 0.73), (7.69, 0.73), (9.53, 0.71), (11.68, 0.76), (13.94, 1.05))
-FILL_AT = (4.45, 12.45, 17.5)
-FILL_STEP = 1.09
+EVENTS = ((1.54, 0.310), (2.88, 0.710), (4.98, 0.730), (7.79, 0.730), (10.14, 0.800), (12.84, 0.840), (18.50, 0.950))
+FILL_AT = (4.45, 12.45, 17.46)
+FILL_STEP = 1.06
 LINE = 4
 
 
@@ -151,7 +151,7 @@
     T, S, sizes,
     x_hbm, co_hbm, k_hbm, gain_ref, bias_ref, ct_hbm,
     gi_ref, gk_ref, gg_ref, gb_ref,
-    xw, co_ref, ct_ref, slice_out, cw, st_out, st_in, own, pre, fx, fg, fbuf,
+    x_ref, xw, co_ref, ct_ref, slice_out, cw, st_out, st_in, own, pre, fx, fg, fbuf,
     gflat, gs, gr, gh, ge_out, ge_in, gown, gw, xt, wbuf, tot, acc, sbuf, rbuf, zbuf,
     in_sem, w_sem, st_send, st_recv, bulk_send, bulk_recv, rs_send, rs_recv, tree_send, tree_recv,
 ):
@@ -171,23 +171,43 @@
 
     loads = [
         pltpu.make_async_copy(src, dst, in_sem.at[i])
-        for i, (src, dst) in enumerate(((co_hbm, co_ref), (ct_hbm, ct_ref), (x_hbm.at[0], xw.at[0, s])))
+        for i, (src, dst) in enumerate(((co_hbm, co_ref), (ct_hbm, ct_ref), (x_hbm, x_ref)))
     ]
     for copy in loads:
         copy.start()
+
+    barrier = pltpu.get_barrier_semaphore()
+
+    strips = S.bit_length() - 1
+    spans = N.bit_length() - 1 - strips
+    flip_s = [(1 - 2 * lax.rem(s // 2**k, 2)) * 2**k for k in range(strips)]
+    flip_t = [(1 - 2 * lax.rem(t // 2**k, 2)) * 2**k for k in range(spans)]
+
+    def others():
+        for r in range(N - 1, 0, -1):
+            to_s = sum((flip for k, flip in enumerate(flip_s) if r >> k & 1), s)
+            to_t = sum((flip for k, flip in enumerate(flip_t) if r >> (k + strips) & 1), t)
+            yield r, (to_t, to_s)
+
+    def each_other(act):
+        if N <= 64:
+            for r, to in others():
+                act(r, to)
+        else:
+            def step(r, carry):
+                r = N - r
+                to_s = sum((lax.rem(r // 2**k, 2) * flip for k, flip in enumerate(flip_s)), s)
+                to_t = sum((lax.rem(r // 2 ** (k + strips), 2) * flip for k, flip in enumerate(flip_t)), t)
+                act(r, (to_t, to_s))
+                return carry
+
+            lax.fori_loop(1, N, step, 0)
+
+    each_other(lambda r, to: pl.semaphore_signal(barrier, inc=1, device_id=to, device_id_type=MESH))
+
+    loads[0].wait()
     load = pltpu.make_async_copy(k_hbm, wbuf, w_sem)
     load.start()
-
-    barrier = pltpu.get_barrier_semaphore()
-
-    def greet(r, carry):
-        d = lax.rem(me + r, N)
-        pl.semaphore_signal(barrier, inc=1, device_id=(d // S, lax.rem(d, S)), device_id_type=MESH)
-        return carry
-
-    lax.fori_loop(1, N, greet, 0)
-
-    loads[0].wait()
     conv = co_ref[0].astype(F32)
     first = jnp.sum(jnp.sum(conv, axis=0), axis=0, keepdims=True)
     second = jnp.sum(jnp.sum(conv * conv, axis=0), axis=0, keepdims=True)
@@ -198,33 +218,21 @@
             st_out[which, halves + i : halves + i + 1, :] = two[:, i * 128 : (i + 1) * 128]
 
     def send_stats(which):
-        def send(r, carry):
-            r = 1 + lax.rem(r + N // 2 - 1, N - 1)
-            d = lax.rem(me + r, N)
-            pltpu.make_async_remote_copy(
-                src_ref=st_out.at[which], dst_ref=st_in.at[which, r - 1],
-                send_sem=st_send.at[which], recv_sem=st_recv.at[which],
-                device_id=(d // S, lax.rem(d, S)), device_id_type=MESH,
-            ).start()
-            return carry
-
-        lax.fori_loop(1, N, send, 0)
+        each_other(lambda r, to: pltpu.make_async_remote_copy(
+            src_ref=st_out.at[which], dst_ref=st_in.at[which, r - 1],
+            send_sem=st_send.at[which], recv_sem=st_recv.at[which],
+            device_id=to, device_id_type=MESH,
+        ).start())
 
     def take_stats(which):
         pltpu.make_async_copy(st_in.at[which], st_in.at[which], st_recv.at[which]).wait()
         return jnp.sum(st_in[which], axis=0) + st_out[which]
 
     put_stats(0, first, second)
+    pl.semaphore_wait(barrier, N - 1)
+    send_stats(0)
     loads[1].wait()
     loads[2].wait()
-    for arr, ref in ((0, co_ref), (1, ct_ref)):
-        whole = ref[0]
-        for j in range(S):
-            slice_out[j, arr] = whole[:, :, j * ce : (j + 1) * ce]
-    keep = pltpu.make_async_copy(slice_out.at[s], cw.at[s], in_sem.at[3])
-    keep.start()
-    pl.semaphore_wait(barrier, N - 1)
-    send_stats(0)
 
     sent = []
 
@@ -258,9 +266,21 @@
     behind = (frame(-1), s)
     has_next, has_before = t + 1 < T, t > 0
     cut, mate, past = [], [], [[], []]
+    def pack(ref):
+        for h in range(rows):
+            gflat[h * cols : (h + 1) * cols, :] = ref[0, h].astype(F32)
+        return gflat[...].astype(BF16)
+
+    xw[0, s] = pack(x_ref)
     past[0].append(push(xw.at[0, s], xw.at[1, s], ahead, has_next))
     for r in range(1, S):
         mate.append(push(xw.at[0, s], xw.at[0, s], (t, strip(-r))))
+    for arr, ref in ((0, co_ref), (1, ct_ref)):
+        whole = pack(ref)
+        for j in range(S):
+            slice_out[j, arr] = whole[:, j * ce : (j + 1) * ce]
+    keep = pltpu.make_async_copy(slice_out.at[s], cw.at[s], in_sem.at[3])
+    keep.start()
     for r in range(1, S):
         cut.append(push(slice_out.at[strip(-r)], cw.at[s], (t, strip(-r))))
 
@@ -341,7 +361,8 @@
             value = xw[k, j].astype(F32)
             if k > 0:
                 value = jnp.where(t >= k, value, 0.0)
-            fx[0:rows, j * cols : (j + 1) * cols, :] = value
+            for h in range(rows):
+                fx[h, j * cols : (j + 1) * cols, :] = value[h * cols : (h + 1) * cols]
         placed = fx[...].reshape(fx.shape[0] * fx.shape[1], chans)[0:depth]
         xt[k] = jnp.transpose(placed).astype(BF16)
 
@@ -383,7 +404,9 @@
 
     seconds = tuple(part(p) for p in (inv, gain, plain, product))
     for j in range(S):
-        fg[1 : rows + 1, j * cols : (j + 1) * cols, :] = conv_grad(pre[j, 0], pre[j, 1], *seconds)
+        value = conv_grad(pre[j, 0], pre[j, 1], *seconds)
+        for h in range(rows):
+            fg[h + 1, j * cols : (j + 1) * cols, :] = value[h * cols : (h + 1) * cols]
     tall = fg.shape[0] * width
     f = fg[...].reshape(tall, ce)
     column = lax.broadcasted_iota(jnp.int32, fg.shape, 1).reshape(tall, ce)
@@ -713,15 +736,16 @@
             in_specs=[hbm, hbm, hbm, vmem, vmem, hbm],
             out_specs=(vmem, vmem, vmem, vmem),
             scratch_shapes=[
-                pltpu.VMEM((3, S, rows, cols, chans), BF16),
+                pltpu.VMEM(conv_input.shape, BF16),
+                pltpu.VMEM((3, S, rows * cols, chans), BF16),
                 pltpu.VMEM(conv_out.shape, BF16),
                 pltpu.VMEM(cotangent.shape, BF16),
-                pltpu.VMEM((S, 2, rows, cols, ce), BF16),
-                pltpu.VMEM((S, 2, rows, cols, ce), BF16),
+                pltpu.VMEM((S, 2, rows * cols, ce), BF16),
+                pltpu.VMEM((S, 2, rows * cols, ce), BF16),
                 pltpu.VMEM((2, 2 * chans // 128, 128), F32),
                 pltpu.VMEM((2, T * S - 1, 2 * chans // 128, 128), F32),
                 pltpu.VMEM((2, rows, cols, chans), F32),
-                pltpu.VMEM((S, 2, rows, cols, ce), F32),
+                pltpu.VMEM((S, 2, rows * cols, ce), F32),
                 pltpu.VMEM((fx_rows, width, chans), F32),
                 pltpu.VMEM((fg_rows, width, ce), F32),
                 pltpu.VMEM((rows + 2, pitch, chans), F32),

time: 55.9 us -> 51.4 us (0.919)
  Pallas kernels: 55.1 us -> 50.6 us
    pallas_call x1, Pallas kernels: 52.7 us -> 48.2 us  [shards(): pl.pallas_call(functools.partial(body, T, S, sizes), out_shape=(pltpu.VME...]
where the time goes in v5:
time: 51.4 us; the launch traced here: 51.3 us
  Pallas kernels  50.6 us (98%)
  between operations  0.64 us (1%)
    pallas_call x1, Pallas kernels, shards(): pl.pallas_call(functools.partial(body, T, S, sizes), out_shape=(pltpu.VME...  48.2 us
    pallas_call x1, Pallas kernels, shards(): pl.pallas_call(hand_out, out_shape=(jax.ShapeDtypeStruct(gi.shape, BF16),...  2.47 us

profile of v5, /device:TPU:0, one launch (start us, length us, event | category | flops | bytes accessed | tf_op | source)
XLA Modules:
  0.0 51.3 jit_solution(16592789249158753584)
XLA Ops:
  0.6 48.2 %shard_map.93 = (bf16[1,12,20,256]{3,2,1,0:T(8,128)(2,1)S(1)}, bf16[6912,128]{1,0:T(8,128)(2,1)S(1)}, f32[1,256]{1,0:T(1,128)S(1)}, f32[1,256]{1,0:T(1,128)S(1)}) custom-call(bf16[1,12,20,256]{3,2,1,0:T(8,128)(2,1)} %x_hbm.1, bf16[1,12,20,256]{3,2,1,0:T(8,128)(2,1)} %co_hbm.1, bf16[3,3,3,256,256]{4,3,2,1,0:T(8,128)(2,1)} %k_hbm.1, f32[1,256]{1,0:T(1,128)} %bitcast.5, ...), custom_call_target="tpu_custom_call" | custom-call | tf_op jit(solution)/shard_map/pallas_call | solution.py:728
  48.8 2.5 %shard_map.94 = (bf16[1,12,20,256]{3,2,1,0:T(8,128)(2,1)}, f32[6912,128]{1,0:T(8,128)}, f32[1,256]{1,0:T(1,128)}, f32[1,256]{1,0:T(1,128)}) custom-call(bf16[1,12,20,256]{3,2,1,0:T(8,128)(2,1)S(1)} %get-tuple-element.12.gi_in, bf16[6912,128]{1,0:T(8,128)(2,1)S(1)} %get-tuple-element.13.gk_in, f32[1,256]{1,0:T(1,128)S(1)} %get-tuple-element.14.gg_in, ...), custom_call_target="tpu_custom_call" | custom-call | tf_op jit(solution)/shard_map/pallas_call | solution.py:782

commit v6 on v5

--- a/solution.py
+++ b/solution.py
@@ -10,7 +10,6 @@
 
 GROUPS = 32
 STREAMS = 13
-PARTS = 3
 EPSILON = 1e-06
 MESH = pl.DeviceIdType.MESH
 F32 = jnp.float32
@@ -33,17 +32,16 @@
     return x
 
 
-def hand_out(gi_in, gk_in, gg_in, gb_in, gi_out, gk_out, gg_out, gb_out, wide, sems):
+PARTS = 1
+
+
+def hand_out(gi_in, gk_in, gg_in, gb_in, gi_out, gk_out, gg_out, gb_out, sems):
     rows = gk_out.shape[0] // PARTS
-    copies = [pltpu.make_async_copy(gi_in, gi_out, sems.at[PARTS])]
-    copies[0].start()
-    for i in range(PARTS):
-        at = slice(i * rows, (i + 1) * rows)
-        wide[at, :] = gk_in[at, :].astype(F32)
-        copies.append(pltpu.make_async_copy(wide.at[at], gk_out.at[at], sems.at[i]))
-        copies[-1].start()
-    gg_out[...] = gg_in[...]
-    gb_out[...] = gb_in[...]
+    pairs = [(gk_in.at[i * rows : (i + 1) * rows], gk_out.at[i * rows : (i + 1) * rows]) for i in range(PARTS)]
+    pairs += [(gi_in, gi_out), (gg_in, gg_out), (gb_in, gb_out)]
+    copies = [pltpu.make_async_copy(src, dst, sems.at[i]) for i, (src, dst) in enumerate(pairs)]
+    for copy in copies:
+        copy.start()
     for copy in copies:
         copy.wait()
 
@@ -150,8 +148,8 @@
 def body(
     T, S, sizes,
     x_hbm, co_hbm, k_hbm, gain_ref, bias_ref, ct_hbm,
-    gi_ref, gk_ref, gg_ref, gb_ref,
-    x_ref, xw, co_ref, ct_ref, slice_out, cw, st_out, st_in, own, pre, fx, fg, fbuf,
+    gi_ref, gk_out, gg_ref, gb_ref,
+    gk_ref, x_ref, xw, co_ref, ct_ref, slice_out, cw, st_out, st_in, own, pre, fx, fg, fbuf,
     gflat, gs, gr, gh, ge_out, ge_in, gown, gw, xt, wbuf, tot, acc, sbuf, rbuf, zbuf,
     in_sem, w_sem, st_send, st_recv, bulk_send, bulk_recv, rs_send, rs_recv, tree_send, tree_recv,
 ):
@@ -464,7 +462,7 @@
         "line": (toward * 4 + lax.rem(t, 4), s),
         "middle": (lax.rem(3 - z + T, T) * 4 + lax.rem(t, 4), s),
     }
-    slots = {"c0": 0, "x0": 1, "z0": 2, "z1": 3, "a2b": 3, "a1": 4, "a2a": 4, "x1": 5}
+    slots = {"c0": 0, "x1": 0, "x0": 1, "a1": 1, "a2a": 1, "z0": 2, "z1": 3, "a2b": 3}
 
     def tree_push(p, kind, src, dst, device):
         by_role = kind in ("z0", "z1", "a1", "a2a", "a2b")
@@ -485,6 +483,10 @@
 
     def rows_of(ref, p, off, n):
         return ref.at[span(p, off, n)]
+
+    def widen(p, off, n):
+        at = span(p, off, n)
+        gk_out[at, :] = gk_ref[at, :].astype(F32)
 
     def tree_event(p, e):
         half, n, h, mine, apart = places(p)
@@ -557,10 +559,13 @@
         else:
             tree_wait(p, "x1", rows_of(gk_ref, p, apart, n))
             put_whole("c1", apart)
+            widen(p, core * half, half)
 
     def tree_end():
         for ref, i in ((gk_ref.at[0 : total_rows // 2], 2), (acc.at[0 : total_rows * 3 // 4], 0)):
             pltpu.make_async_copy(ref, ref, tree_send.at[i]).wait()
+        for p in range(streams):
+            widen(p, (1 - core) * (sizes[p] // 2), sizes[p] // 2)
 
         @pl.when(outer)
         def _():
@@ -692,6 +697,8 @@
             input_grad(*task[1:])
     if tree:
         tree_end()
+    else:
+        gk_out[...] = gk_ref[...].astype(F32)
 
     for copy in copies:
         copy.wait_send()
@@ -722,20 +729,21 @@
         fg_rows = max(rows + 2, (2 * width + depth + width - 1) // width)
         n_bulk = (S - 1) * 2 + 2 * S + 5 + 6
         tree = T == 4 * LINE
-        halving, line = ((1, 1, 1), (streams, 6)) if tree else ((2, streams, bits), (1, 1))
+        halving, line = ((1, 1, 1), (streams, 4)) if tree else ((2, streams, bits), (1, 1))
         vmem = pl.BlockSpec(memory_space=pltpu.VMEM)
         hbm = pl.BlockSpec(memory_space=pltpu.HBM)
         gi, gk, gg, gb = pl.pallas_call(
             functools.partial(body, T, S, sizes),
             out_shape=(
                 pltpu.VMEM(conv_input.shape, BF16),
-                pltpu.VMEM((total_rows, ce), BF16),
+                pltpu.VMEM((total_rows, ce), F32),
                 pltpu.VMEM((1, chans), F32),
                 pltpu.VMEM((1, chans), F32),
             ),
             in_specs=[hbm, hbm, hbm, vmem, vmem, hbm],
             out_specs=(vmem, vmem, vmem, vmem),
             scratch_shapes=[
+                pltpu.VMEM((total_rows, ce), BF16),
                 pltpu.VMEM(conv_input.shape, BF16),
                 pltpu.VMEM((3, S, rows * cols, chans), BF16),
                 pltpu.VMEM(conv_out.shape, BF16),
@@ -788,8 +796,8 @@
                 jax.ShapeDtypeStruct((1, chans), F32),
             ),
             in_specs=[vmem, vmem, vmem, vmem],
-            out_specs=(hbm, hbm, vmem, vmem),
-            scratch_shapes=[pltpu.VMEM((27 * chans, ce), F32), pltpu.SemaphoreType.DMA((PARTS + 1,))],
+            out_specs=(hbm, hbm, hbm, hbm),
+            scratch_shapes=[pltpu.SemaphoreType.DMA((PARTS + 3,))],
             compiler_params=pltpu.CompilerParams(vmem_limit_bytes=16 * 1024 * 1024),
         )(gi, gk, gg, gb)
         return gi, gk.reshape(3, 3, 3, chans, ce), gg.reshape(chans), gb.reshape(chans)

time: 51.4 us -> 50.8 us (0.988)
  Pallas kernels: 50.6 us -> 50 us
    pallas_call x1, Pallas kernels: 2.47 us -> 1.87 us  [shards(): pl.pallas_call(hand_out, out_shape=(jax.ShapeDtypeStruct(gi.shape, BF16),...]
where the time goes in v6:
time: 50.8 us; the launch traced here: 50.6 us
  Pallas kernels  50 us (98%)
  between operations  0.64 us (1%)
    pallas_call x1, Pallas kernels, shards(): pl.pallas_call(functools.partial(body, T, S, sizes), out_shape=(pltpu.VME...  48.1 us
    pallas_call x1, Pallas kernels, shards(): pl.pallas_call(hand_out, out_shape=(jax.ShapeDtypeStruct(gi.shape, BF16),...  1.87 us

profile of v6, /device:TPU:0, one launch (start us, length us, event | category | flops | bytes accessed | tf_op | source)
XLA Modules:
  0.0 50.6 jit_solution(18345381338348922976)
XLA Ops:
  0.6 48.1 %shard_map.93 = (bf16[1,12,20,256]{3,2,1,0:T(8,128)(2,1)S(1)}, f32[6912,128]{1,0:T(8,128)S(1)}, f32[1,256]{1,0:T(1,128)S(1)}, f32[1,256]{1,0:T(1,128)S(1)}) custom-call(bf16[1,12,20,256]{3,2,1,0:T(8,128)(2,1)} %x_hbm.1, bf16[1,12,20,256]{3,2,1,0:T(8,128)(2,1)} %co_hbm.1, bf16[3,3,3,256,256]{4,3,2,1,0:T(8,128)(2,1)} %k_hbm.1, f32[1,256]{1,0:T(1,128)} %bitcast.5, ...), custom_call_target="tpu_custom_call" | custom-call | tf_op jit(solution)/shard_map/pallas_call | solution.py:735
  48.7 1.9 %shard_map.94 = (bf16[1,12,20,256]{3,2,1,0:T(8,128)(2,1)}, f32[6912,128]{1,0:T(8,128)}, f32[1,256]{1,0:T(1,128)}, f32[1,256]{1,0:T(1,128)}) custom-call(bf16[1,12,20,256]{3,2,1,0:T(8,128)(2,1)S(1)} %get-tuple-element.12.gi_in, f32[6912,128]{1,0:T(8,128)S(1)} %get-tuple-element.13.gk_in, f32[1,256]{1,0:T(1,128)S(1)} %get-tuple-element.14.gg_in, ...), custom_call_target="tpu_custom_call" | custom-call | tf_op jit(solution)/shard_map/pallas_call | solution.py:790

commit v7 on v6

--- a/solution.py
+++ b/solution.py
@@ -150,7 +150,7 @@
     x_hbm, co_hbm, k_hbm, gain_ref, bias_ref, ct_hbm,
     gi_ref, gk_out, gg_ref, gb_ref,
     gk_ref, x_ref, xw, co_ref, ct_ref, slice_out, cw, st_out, st_in, own, pre, fx, fg, fbuf,
-    gflat, gs, gr, gh, ge_out, ge_in, gown, gw, xt, wbuf, tot, acc, sbuf, rbuf, zbuf,
+    gflat, gs, gh, ge_out, ge_in, gown, gw, xt, wbuf, tot, acc, sbuf, rbuf, zbuf,
     in_sem, w_sem, st_send, st_recv, bulk_send, bulk_recv, rs_send, rs_recv, tree_send, tree_recv,
 ):
     N = T * S
@@ -388,8 +388,7 @@
         ge_out[1, h : h + 1, :] = g[h, cols - 1 : cols, :].astype(BF16)
     second = (frame(-2), s)
     later = {
-        "pair": push(gs, gr, ahead, even),
-        "near": push(gs, gh.at[0], behind, odd),
+        "near": push(gs, gh.at[0], behind, has_before),
         "far": push(gs, gh.at[1], second, odd & (t > 1)),
     }
     rims = []
@@ -535,9 +534,9 @@
             def _():
                 tree_wait(p, "z1", zbuf.at[zrow])
                 gk_ref[span(p, near, h), :] = (taken(acc, near, h) + zbuf[zrow, :].astype(F32)).astype(BF16)
-                put_half("x1", near, mates["x"])
                 put_half("a1", near, mates["middle"])
                 put_half("a2a", near, mates["line"])
+                put_half("x1", near, mates["x"])
         elif e == 4:
             @pl.when(inner)
             def _():
@@ -635,9 +634,6 @@
             acc[at : at + chans, :] = res[:, c * ce : (c + 1) * ce]
         for p in ready:
             begin(p)
-        if (a, b) == (TAPS_A[0], 2):
-            take(later["pair"], gr, odd)
-            later["next"] = push(gr, gh.at[0], second, odd & (t > 1))
 
     def put_gown(k):
         live = t + k < T
@@ -645,8 +641,7 @@
             value = gs[...].astype(F32)
         else:
             if k == 1:
-                take(later["near"], gh.at[0], live & even)
-                take(later["next"], gh.at[0], live & odd)
+                take(later["near"], gh.at[0], live)
                 later["last"] = push(gh.at[0], gh.at[1], behind, live & odd)
             else:
                 take(later["far"], gh.at[1], live & odd)
@@ -727,7 +722,7 @@
         depth = round_up(rows * width, 128)
         fx_rows = (depth + width - 1) // width
         fg_rows = max(rows + 2, (2 * width + depth + width - 1) // width)
-        n_bulk = (S - 1) * 2 + 2 * S + 5 + 6
+        n_bulk = (S - 1) * 2 + 2 * S + 3 + 6
         tree = T == 4 * LINE
         halving, line = ((1, 1, 1), (streams, 4)) if tree else ((2, streams, bits), (1, 1))
         vmem = pl.BlockSpec(memory_space=pltpu.VMEM)
@@ -758,7 +753,6 @@
                 pltpu.VMEM((fg_rows, width, ce), F32),
                 pltpu.VMEM((rows + 2, pitch, chans), F32),
                 pltpu.VMEM((rows * cols, chans), F32),
-                pltpu.VMEM((rows * cols, chans), BF16),
                 pltpu.VMEM((rows * cols, chans), BF16),
                 pltpu.VMEM((2, rows * cols, chans), BF16),
                 pltpu.VMEM((2, rows, chans), BF16),

time: 50.8 us -> 51 us (level)
  no operation moved by 1% of the time
where the time goes in v7:
time: 51 us; the launch traced here: 50.8 us
  Pallas kernels  50.2 us (98%)
  between operations  0.64 us (1%)
    pallas_call x1, Pallas kernels, shards(): pl.pallas_call(functools.partial(body, T, S, sizes), out_shape=(pltpu.VME...  48.3 us
    pallas_call x1, Pallas kernels, shards(): pl.pallas_call(hand_out, out_shape=(jax.ShapeDtypeStruct(gi.shape, BF16),...  1.87 us

profile of v7, /device:TPU:0, one launch (start us, length us, event | category | flops | bytes accessed | tf_op | source)
XLA Modules:
  0.0 50.8 jit_solution(12014755444985156868)
XLA Ops:
  0.6 48.3 %shard_map.93 = (bf16[1,12,20,256]{3,2,1,0:T(8,128)(2,1)S(1)}, f32[6912,128]{1,0:T(8,128)S(1)}, f32[1,256]{1,0:T(1,128)S(1)}, f32[1,256]{1,0:T(1,128)S(1)}) custom-call(bf16[1,12,20,256]{3,2,1,0:T(8,128)(2,1)} %x_hbm.1, bf16[1,12,20,256]{3,2,1,0:T(8,128)(2,1)} %co_hbm.1, bf16[3,3,3,256,256]{4,3,2,1,0:T(8,128)(2,1)} %k_hbm.1, f32[1,256]{1,0:T(1,128)} %bitcast.5, ...), custom_call_target="tpu_custom_call" | custom-call | tf_op jit(solution)/shard_map/pallas_call | solution.py:730
  48.9 1.9 %shard_map.94 = (bf16[1,12,20,256]{3,2,1,0:T(8,128)(2,1)}, f32[6912,128]{1,0:T(8,128)}, f32[1,256]{1,0:T(1,128)}, f32[1,256]{1,0:T(1,128)}) custom-call(bf16[1,12,20,256]{3,2,1,0:T(8,128)(2,1)S(1)} %get-tuple-element.12.gi_in, f32[6912,128]{1,0:T(8,128)S(1)} %get-tuple-element.13.gk_in, f32[1,256]{1,0:T(1,128)S(1)} %get-tuple-element.14.gg_in, ...), custom_call_target="tpu_custom_call" | custom-call | tf_op jit(solution)/shard_map/pallas_call | solution.py:784
